TPU v7x, 512 devices: a whole 4x8x8 slice. The times are simulated.
512 devices in a mesh: chan: 16 (over y, core), tm: 32 (over z, x).
Axes of the slice: x: 4, y: 8, z: 8, core: 2. Of those that a mesh axis runs over, the one named last changes fastest.
Arguments:
- signal: float32 [256, 131072], P('chan', 'tm'), may hold values from -80 to 80
- filters: float32 [16, 131072], P(None, 'tm'), may hold values from -6 to 6
- gate_scale: float32 [256], P('chan'), may hold values from 0.5 to 2
- gate_shift: float32 [256], P('chan'), may hold values from -3 to 3
Outputs:
- predicted: float32 [256, 131072], P('chan', 'tm')
- grad_filter: float32 [16, 131072], P(None, 'tm')
- mean_loss: float32 [], replicated
All inputs are finite; a program needn't handle non-finite values.
Results may differ from a plain program's by a relative error of at most 0.0003.
Values sent between devices are 32-bit elements; how exact they have to be, the bound alone decides.
A program may use at most 64 MiB of HBM per device.

v0:
```python
import math

import jax
import jax.numpy as jnp
import numpy as np
from jax import lax
from jax.sharding import PartitionSpec as P

CHANNELS = 256


var_floor = 1.0
highest = lax.Precision.HIGHEST


def entering(value, axis, join, neutral):
    count, mine = (lax.axis_size(axis), lax.axis_index(axis))
    pieces = jax.tree.map(lambda part: lax.all_gather(part, axis), value)
    so_far = jax.tree.map(
        lambda part, zero: jnp.full_like(part, 0) + jnp.asarray(zero, part.dtype), value, neutral
    )

    def hop(position, so_far):
        longer = join(so_far, jax.tree.map(lambda part: part[position], pieces))
        return jax.tree.map(lambda new, old: jnp.where(position < mine, new, old), longer, so_far)

    return lax.fori_loop(0, count - 1, hop, so_far)


def passed_along(shard, axis, by):
    length = lax.axis_size(axis)
    pairs = [(i, i + by) for i in range(length) if 0 <= i + by < length]
    return lax.ppermute(shard, axis, pairs)


def matmul(first_op, second_op):
    return jnp.dot(first_op, second_op, precision=highest, preferred_element_type=jnp.float32)


def build_tables(length_here, shards, position, freq_order):
    slice_len = length_here // shards
    total_len = 2 * shards * length_here
    inner_size = min(128, length_here)
    outer_size = length_here // inner_size
    two_pi = 2.0 * math.pi
    freq_idx = jnp.asarray(freq_order, jnp.int32)
    source_idx = jnp.arange(shards, dtype=jnp.int32)
    angle_cross = (
        two_pi
        / (2 * shards)
        * (freq_idx[:, None] * source_idx[None, :] % (2 * shards)).astype(jnp.float32)
    )
    slice_idx = position * slice_len + jnp.arange(slice_len, dtype=jnp.int32)
    angle_twist = (
        two_pi
        / total_len
        * (freq_idx[:, None] * slice_idx[None, :] % total_len).astype(jnp.float32)
    )
    outer_idx = jnp.arange(outer_size, dtype=jnp.int32)
    inner_idx = jnp.arange(inner_size, dtype=jnp.int32)
    angle_outer = (
        two_pi
        / outer_size
        * (outer_idx[:, None] * outer_idx[None, :] % outer_size).astype(jnp.float32)
    )
    angle_middle = (
        two_pi
        / length_here
        * (outer_idx[:, None] * inner_idx[None, :] % length_here).astype(jnp.float32)
    )
    angle_inner = (
        two_pi
        / inner_size
        * (inner_idx[:, None] * inner_idx[None, :] % inner_size).astype(jnp.float32)
    )
    return (
        jnp.cos(angle_cross),
        jnp.sin(angle_cross),
        jnp.cos(angle_twist)[:, None, :],
        jnp.sin(angle_twist)[:, None, :],
        jnp.cos(angle_outer),
        jnp.sin(angle_outer),
        jnp.cos(angle_middle),
        jnp.sin(angle_middle),
        jnp.cos(angle_inner),
        jnp.sin(angle_inner),
    )


def local_forward(flat_real, flat_imag, tables):
    cos_outer, sin_outer, cos_middle, sin_middle, cos_inner, sin_inner = tables[4:]
    row_total, length_here = flat_real.shape
    outer_size = cos_outer.shape[0]
    inner_size = cos_inner.shape[0]
    grid_real = flat_real.reshape(row_total, outer_size, inner_size)
    grid_imag = flat_imag.reshape(row_total, outer_size, inner_size)
    first_real = jnp.einsum("ca,rab->rcb", cos_outer, grid_real, precision=highest) + jnp.einsum(
        "ca,rab->rcb", sin_outer, grid_imag, precision=highest
    )
    first_imag = jnp.einsum("ca,rab->rcb", cos_outer, grid_imag, precision=highest) - jnp.einsum(
        "ca,rab->rcb", sin_outer, grid_real, precision=highest
    )
    turned_real = first_real * cos_middle + first_imag * sin_middle
    turned_imag = first_imag * cos_middle - first_real * sin_middle
    final_real = matmul(turned_real, cos_inner) + matmul(turned_imag, sin_inner)
    final_imag = matmul(turned_imag, cos_inner) - matmul(turned_real, sin_inner)
    return (final_real.reshape(row_total, length_here), final_imag.reshape(row_total, length_here))


def local_inverse(spec_real, spec_imag, tables):
    cos_outer, sin_outer, cos_middle, sin_middle, cos_inner, sin_inner = tables[4:]
    row_total, length_here = spec_real.shape
    outer_size = cos_outer.shape[0]
    inner_size = cos_inner.shape[0]
    grid_real = spec_real.reshape(row_total, outer_size, inner_size)
    grid_imag = spec_imag.reshape(row_total, outer_size, inner_size)
    first_real = matmul(grid_real, cos_inner) - matmul(grid_imag, sin_inner)
    first_imag = matmul(grid_imag, cos_inner) + matmul(grid_real, sin_inner)
    turned_real = first_real * cos_middle - first_imag * sin_middle
    turned_imag = first_imag * cos_middle + first_real * sin_middle
    final_real = jnp.einsum("ca,rcb->rab", cos_outer, turned_real, precision=highest) - jnp.einsum(
        "ca,rcb->rab", sin_outer, turned_imag, precision=highest
    )
    final_imag = jnp.einsum("ca,rcb->rab", cos_outer, turned_imag, precision=highest) + jnp.einsum(
        "ca,rcb->rab", sin_outer, turned_real, precision=highest
    )
    return (final_real.reshape(row_total, length_here), final_imag.reshape(row_total, length_here))


def forward_spectrum(values, tables, shards):
    cos_cross, sin_cross, cos_twist, sin_twist = tables[:4]
    count_rows, length_here = values.shape
    slice_len = length_here // shards
    pieces = lax.all_to_all(
        values.reshape(count_rows, shards, slice_len), "tm", split_axis=1, concat_axis=1, tiled=True
    )
    cross_real = jnp.einsum("kq,rqs->krs", cos_cross, pieces, precision=highest)
    cross_imag = -jnp.einsum("kq,rqs->krs", sin_cross, pieces, precision=highest)
    twist_real = cross_real * cos_twist + cross_imag * sin_twist
    twist_imag = cross_imag * cos_twist - cross_real * sin_twist
    shape_four = (2 * shards, count_rows, 1, slice_len)
    got_real, got_imag = (
        lax.all_to_all(
            twist_real.reshape(shape_four), "tm", split_axis=0, concat_axis=2, tiled=True
        ),
        lax.all_to_all(
            twist_imag.reshape(shape_four), "tm", split_axis=0, concat_axis=2, tiled=True
        ),
    )
    final_real, final_imag = local_forward(
        got_real.reshape(2 * count_rows, length_here),
        got_imag.reshape(2 * count_rows, length_here),
        tables,
    )
    return (final_real, final_imag)


def inverse_real(spec_real, spec_imag, tables, shards):
    cos_cross, sin_cross, cos_twist, sin_twist = tables[:4]
    paired_rows, length_here = spec_real.shape
    count_rows = paired_rows // 2
    slice_len = length_here // shards
    total_len = 2 * shards * length_here
    wave_real, wave_imag = local_inverse(spec_real, spec_imag, tables)
    shape_four = (2, count_rows, shards, slice_len)
    back_real, back_imag = (
        lax.all_to_all(
            wave_real.reshape(shape_four), "tm", split_axis=2, concat_axis=0, tiled=True
        ),
        lax.all_to_all(
            wave_imag.reshape(shape_four), "tm", split_axis=2, concat_axis=0, tiled=True
        ),
    )
    back_real = back_real.reshape(2 * shards, count_rows, slice_len)
    back_imag = back_imag.reshape(2 * shards, count_rows, slice_len)
    turned_real = back_real * cos_twist - back_imag * sin_twist
    turned_imag = back_imag * cos_twist + back_real * sin_twist
    joined = (
        jnp.einsum("kq,krs->rqs", cos_cross, turned_real, precision=highest)
        - jnp.einsum("kq,krs->rqs", sin_cross, turned_imag, precision=highest)
    ) / total_len
    merged = lax.all_to_all(joined, "tm", split_axis=1, concat_axis=1, tiled=True)
    return merged.reshape(count_rows, length_here)


def add_pair(earlier, latter):
    return (earlier[0] + latter[0], earlier[1] + latter[1])


def per_device(signal, filters, gate_scale, gate_shift):
    channels_here, length_here = signal.shape
    filter_count = filters.shape[0]
    groups_here = channels_here // filter_count
    shards = lax.axis_size("tm")
    position = lax.axis_index("tm")
    full_length = shards * length_here
    tap_scale = 1.0 / math.sqrt(full_length)
    freq_order = np.arange(2 * shards).astype(np.int32)
    tables = build_tables(length_here, shards, position, freq_order)
    sum_first = jnp.sum(signal, axis=1)
    sum_second = jnp.sum(signal * signal, axis=1)
    zero_row = jnp.zeros((channels_here,), jnp.float32)
    before_first, before_second = entering(
        (sum_first, sum_second), "tm", add_pair, (zero_row, zero_row)
    )
    steps_here = position * length_here + jnp.arange(length_here, dtype=jnp.int32)
    counts = (steps_here + 1).astype(jnp.float32)
    running_mean = (before_first[:, None] + jnp.cumsum(signal, axis=1)) / counts
    running_var = (
        before_second[:, None] + jnp.cumsum(signal * signal, axis=1)
    ) / counts - running_mean * running_mean
    spread = jnp.sqrt(jnp.maximum(running_var, var_floor))
    normed = (signal - running_mean) / spread
    gating = jax.nn.sigmoid(gate_scale[:, None] * normed + gate_shift[:, None])
    taps = filters * tap_scale
    rows_all = channels_here + filter_count
    spec_real, spec_imag = forward_spectrum(jnp.concatenate([normed, taps], axis=0), tables, shards)
    spec_real = spec_real.reshape(2, rows_all, length_here)
    spec_imag = spec_imag.reshape(2, rows_all, length_here)
    norm_real = spec_real[:, :channels_here].reshape(2, groups_here, filter_count, length_here)
    norm_imag = spec_imag[:, :channels_here].reshape(2, groups_here, filter_count, length_here)
    filt_real = spec_real[:, channels_here:][:, None]
    filt_imag = spec_imag[:, channels_here:][:, None]
    prod_real = norm_real * filt_real - norm_imag * filt_imag
    prod_imag = norm_real * filt_imag + norm_imag * filt_real
    mixed_conv = inverse_real(
        prod_real.reshape(2 * channels_here, length_here),
        prod_imag.reshape(2 * channels_here, length_here),
        tables,
        shards,
    )
    predicted = signal + spread * mixed_conv * gating
    following = passed_along(signal[:, :1], "tm", -1)
    target = jnp.concatenate([signal[:, 1:], following], axis=1)
    residual = jnp.where((steps_here < full_length - 1)[None, :], predicted - target, 0.0)
    error_sum = lax.psum(jnp.sum(residual * residual), ("chan", "tm"))
    mean_loss = error_sum / (CHANNELS * (full_length - 1))
    upstream = 2.0 / CHANNELS * residual * spread * gating
    up_real, up_imag = forward_spectrum(upstream, tables, shards)
    up_real = up_real.reshape(2, groups_here, filter_count, length_here)
    up_imag = up_imag.reshape(2, groups_here, filter_count, length_here)
    cross_real = jnp.sum(up_real * norm_real + up_imag * norm_imag, axis=1)
    cross_imag = jnp.sum(up_imag * norm_real - up_real * norm_imag, axis=1)
    local_grad = inverse_real(
        cross_real.reshape(2 * filter_count, length_here),
        cross_imag.reshape(2 * filter_count, length_here),
        tables,
        shards,
    )
    grad_filter = lax.psum(local_grad * tap_scale, "chan")
    return (predicted, grad_filter, mean_loss)


def solution(mesh):
    return jax.shard_map(
        per_device,
        mesh=mesh,
        in_specs=(P("chan", "tm"), P(None, "tm"), P("chan"), P("chan")),
        out_specs=(P("chan", "tm"), P(None, "tm"), P()),
        check_vma=False,
    )
```

profile of v0, /device:TPU:1, one launch (start us, length us, event | category | flops | bytes accessed | tf_op | source)
XLA Modules:
  0.0 518.6 jit_solution(490203820335122200)
XLA Ops:
  10.7 67.5 %all-reduce.2 = (f32[512]{0:T(512)S(1)}, f32[512]{0:T(512)S(1)}) all-reduce(f32[512]{0:T(512)S(1)} %dynamic-update-slice, f32[512]{0:T(512)S(1)} %dynamic-update-slice.1), channel_id=2, replica_groups=mesh['chan'=16,'tm'=32] {'tm'}, use_global_device_ids=true, to_apply=%add | all-reduce | flops 1024 | bytes 8192
  79.7 4.6 reduce-window.14
  85.8 4.6 reduce-window.16
  93.8 3.9 all-to-all-start
  97.8 12.8 %all-to-all-done = f32[32,32,128]{2,0,1:T(8,128)S(1)} async-done(((f32[32,32,128]{2,0,1:T(8,128)}), f32[32,32,128]{2,0,1:T(8,128)S(1)}, u32[]{:S(2)}, u32[]{:S(2)}) %all-to-all-start) | async-done | bytes 524320 | tf_op jit(solution)/shard_map/all_to_all | solution.py:134
  115.0 3.9 all-to-all-start.2
  120.6 15.8 %all-to-all-done.2 = f32[64,32,1,128]{3,1,2,0:T(8,128)S(1)} async-done(((f32[64,32,1,128]{3,1,2,0:T(8,128)}), f32[64,32,1,128]{3,1,2,0:T(8,128)S(1)}, u32[]{:S(2)}, u32[]{:S(2)}) %all-to-all-start.2) | async-done | bytes 1048608 | tf_op jit(solution)/shard_map/all_to_all | solution.py:146
  136.4 5.1 all-to-all-start.1
  144.3 19.7 %all-to-all-done.1 = f32[64,32,1,128]{3,1,2,0:T(8,128)S(1)} async-done(((f32[64,32,1,128]{3,1,2,0:T(8,128)}), f32[64,32,1,128]{3,1,2,0:T(8,128)S(1)}, u32[]{:S(2)}, u32[]{:S(2)}) %all-to-all-start.1) | async-done | bytes 1048608 | tf_op jit(solution)/shard_map/all_to_all | solution.py:143
  169.3 2.2 fusion.26
  171.5 2.2 convolution_add_fusion
  175.1 3.4 convolution_subtract_fusion
  186.6 5.3 %all-to-all-start.3 = ((f32[2,16,32,128]{3,1,0,2:T(8,128)}), f32[2,16,32,128]{3,1,0,2:T(8,128)}, u32[]{:S(2)}, u32[]{:S(2)}) async-start(f32[2,16,32,128]{3,1,0,2:T(8,128)} %copy.81), calls=%async_computation.3 | async-start | bytes 1048576 | tf_op jit(solution)/shard_map/all_to_all | solution.py:167
  194.5 10.1 %all-to-all-done.3 = f32[2,16,32,128]{3,1,0,2:T(8,128)} async-done(((f32[2,16,32,128]{3,1,0,2:T(8,128)}), f32[2,16,32,128]{3,1,0,2:T(8,128)}, u32[]{:S(2)}, u32[]{:S(2)}) %all-to-all-start.3) | async-done | bytes 524320 | tf_op jit(solution)/shard_map/all_to_all | solution.py:167
  204.6 4.1 all-to-all-start.4
  210.0 11.8 %all-to-all-done.4 = f32[2,16,32,128]{3,1,0,2:T(8,128)S(1)} async-done(((f32[2,16,32,128]{3,1,0,2:T(8,128)}), f32[2,16,32,128]{3,1,0,2:T(8,128)S(1)}, u32[]{:S(2)}, u32[]{:S(2)}) %all-to-all-start.4) | async-done | bytes 524320 | tf_op jit(solution)/shard_map/all_to_all | solution.py:170
  224.0 6.5 %all-to-all-start.5 = ((f32[16,32,128]{2,0,1:T(8,128)}), f32[16,32,128]{2,0,1:T(8,128)}, u32[]{:S(2)}, u32[]{:S(2)}) async-start(f32[16,32,128]{2,0,1:T(8,128)} %copy.85), calls=%async_computation.5 | async-start | bytes 524288 | tf_op jit(solution)/shard_map/all_to_all | solution.py:182
  232.0 2.9 collective-permute-done
  234.9 6.1 %all-to-all-done.5 = f32[16,32,128]{2,0,1:T(8,128)} async-done(((f32[16,32,128]{2,0,1:T(8,128)}), f32[16,32,128]{2,0,1:T(8,128)}, u32[]{:S(2)}, u32[]{:S(2)}) %all-to-all-start.5) | async-done | bytes 262176 | tf_op jit(solution)/shard_map/all_to_all | solution.py:182
  243.8 15.5 %all_to_all.140 = f32[16,32,128]{2,0,1:T(8,128)S(1)} all-to-all(f32[16,32,128]{2,0,1:T(8,128)S(1)} %copy_bitcast_fusion.2), channel_id=1, replica_groups=mesh['chan'=16,'tm'=32] {'tm'}, dimensions={1} | all-to-all | bytes 524288 | tf_op jit(solution)/shard_map/all_to_all | solution.py:134
  261.9 3.9 all-to-all-start.7
  266.9 11.8 %all-to-all-done.7 = f32[64,16,1,128]{3,1,2,0:T(8,128)S(1)} async-done(((f32[64,16,1,128]{3,1,2,0:T(8,128)}), f32[64,16,1,128]{3,1,2,0:T(8,128)S(1)}, u32[]{:S(2)}, u32[]{:S(2)}) %all-to-all-start.7) | async-done | bytes 524320 | tf_op jit(solution)/shard_map/all_to_all | solution.py:143
  278.7 4.8 all-to-all-start.8
  285.4 10.9 %all-to-all-done.8 = f32[64,16,1,128]{3,1,2,0:T(8,128)} async-done(((f32[64,16,1,128]{3,1,2,0:T(8,128)}), f32[64,16,1,128]{3,1,2,0:T(8,128)}, u32[]{:S(2)}, u32[]{:S(2)}) %all-to-all-start.8) | async-done | bytes 524320 | tf_op jit(solution)/shard_map/all_to_all | solution.py:146
  306.1 2.7 convolution_add_fusion.4
  316.5 3.9 all-to-all-start.9
  323.0 10.3 %all-to-all-done.9 = f32[2,16,32,128]{3,0,1,2:T(2,128)S(1)} async-done(((f32[2,16,32,128]{3,0,1,2:T(2,128)}), f32[2,16,32,128]{3,0,1,2:T(2,128)S(1)}, u32[]{:S(2)}, u32[]{:S(2)}) %all-to-all-start.9) | async-done | bytes 524320 | tf_op jit(solution)/shard_map/all_to_all | solution.py:167
  333.3 3.9 all-to-all-start.10
  337.5 12.6 %all-to-all-done.10 = f32[2,16,32,128]{3,0,1,2:T(2,128)S(1)} async-done(((f32[2,16,32,128]{3,0,1,2:T(2,128)}), f32[2,16,32,128]{3,0,1,2:T(2,128)S(1)}, u32[]{:S(2)}, u32[]{:S(2)}) %all-to-all-start.10) | async-done | bytes 524320 | tf_op jit(solution)/shard_map/all_to_all | solution.py:170
  351.7 14.1 %all_to_all.141 = f32[16,32,128]{2,0,1:T(8,128)S(1)} all-to-all(f32[16,32,128]{2,0,1:T(8,128)S(1)} %copy.102), channel_id=1, replica_groups=mesh['chan'=16,'tm'=32] {'tm'}, dimensions={1} | all-to-all | bytes 524288 | tf_op jit(solution)/shard_map/all_to_all | solution.py:182
  366.5 128.7 %psum.15 = f32[]{:T(128)} all-reduce(f32[]{:T(128)} %get-tuple-element.152), channel_id=1, replica_groups=mesh['chan'=16,'tm'=32] {'chan','tm'}, use_global_device_ids=true, to_apply=%region_10.11 | all-reduce | flops 1 | bytes 8 | tf_op jit(solution)/shard_map/psum | solution.py:236
  495.9 12.8 %all-reduce.5.cloned.1.call-done = f32[16,4096]{1,0:T(8,128)} async-done(((f32[16,4096]{1,0:T(8,128)}), f32[16,4096]{1,0:T(8,128)}) %all-reduce.5.cloned.1.call-update) | async-done | bytes 262160 | tf_op jit(solution)/shard_map/psum | solution.py:250
  (161 shorter events, 73.3 us)
Async XLA Ops:
  84.8 1.0 copy-start
  84.9 6.9 %copy-start.3 = (f32[16,32,128]{2,1,0:T(8,128)}, f32[16,32,128]{2,1,0:T(8,128)S(1)}, u32[]{:S(2)}) copy-start(f32[16,32,128]{2,1,0:T(8,128)S(1)} %broadcast_add_fusion.1) | copy-start | bytes 786436
  90.8 1.0 copy-start.12
  91.8 0.7 copy-start.5
  92.9 0.9 copy-start.8
  93.8 16.8 %all-to-all-start = ((f32[32,32,128]{2,0,1:T(8,128)}), f32[32,32,128]{2,0,1:T(8,128)S(1)}, u32[]{:S(2)}, u32[]{:S(2)}) async-start(f32[32,32,128]{2,0,1:T(8,128)} %copy_bitcast_fusion), calls=%async_computation | async-start | bytes 1048576 | tf_op jit(solution)/shard_map/all_to_all | solution.py:134
  115.0 21.3 %all-to-all-start.2 = ((f32[64,32,1,128]{3,1,2,0:T(8,128)}), f32[64,32,1,128]{3,1,2,0:T(8,128)S(1)}, u32[]{:S(2)}, u32[]{:S(2)}) async-start(f32[64,32,1,128]{3,1,2,0:T(8,128)} %copy.76), calls=%async_computation.2 | async-start | bytes 2097152 | tf_op jit(solution)/shard_map/all_to_all | solution.py:146
  136.4 27.6 %all-to-all-start.1 = ((f32[64,32,1,128]{3,1,2,0:T(8,128)}), f32[64,32,1,128]{3,1,2,0:T(8,128)S(1)}, u32[]{:S(2)}, u32[]{:S(2)}) async-start(f32[64,32,1,128]{3,1,2,0:T(8,128)} %copy.73), calls=%async_computation.1 | async-start | bytes 2097152 | tf_op jit(solution)/shard_map/all_to_all | solution.py:143
  164.6 1.2 copy-start.7
  186.6 18.0 %all-to-all-start.3 = ((f32[2,16,32,128]{3,1,0,2:T(8,128)}), f32[2,16,32,128]{3,1,0,2:T(8,128)}, u32[]{:S(2)}, u32[]{:S(2)}) async-start(f32[2,16,32,128]{3,1,0,2:T(8,128)} %copy.81), calls=%async_computation.3 | async-start | bytes 1048576 | tf_op jit(solution)/shard_map/all_to_all | solution.py:167
  204.6 17.2 %all-to-all-start.4 = ((f32[2,16,32,128]{3,1,0,2:T(8,128)}), f32[2,16,32,128]{3,1,0,2:T(8,128)S(1)}, u32[]{:S(2)}, u32[]{:S(2)}) async-start(f32[2,16,32,128]{3,1,0,2:T(8,128)} %copy.83), calls=%async_computation.4 | async-start | bytes 1048576 | tf_op jit(solution)/shard_map/all_to_all | solution.py:170
  223.2 17.8 %copy-start.13 = (f32[16]{0:T(128)S(1)}, f32[16]{0:T(128)}, u32[]{:S(2)}) copy-start(f32[16]{0:T(128)} %param.10) | copy-start | bytes 196
  223.2 17.8 %copy-start.14 = (f32[16]{0:T(128)S(1)}, f32[16]{0:T(128)}, u32[]{:S(2)}) copy-start(f32[16]{0:T(128)} %param.9) | copy-start | bytes 196
  224.0 17.0 %copy-start.9 = (f32[16,4096]{1,0:T(8,128)S(1)}, f32[16,4096]{1,0:T(8,128)}, u32[]{:S(2)}) copy-start(f32[16,4096]{1,0:T(8,128)} %copy-done.8) | copy-start | bytes 786436
  224.0 17.0 %all-to-all-start.5 = ((f32[16,32,128]{2,0,1:T(8,128)}), f32[16,32,128]{2,0,1:T(8,128)}, u32[]{:S(2)}, u32[]{:S(2)}) async-start(f32[16,32,128]{2,0,1:T(8,128)} %copy.85), calls=%async_computation.5 | async-start | bytes 524288 | tf_op jit(solution)/shard_map/all_to_all | solution.py:182
  230.5 4.4 collective-permute-start
  231.8 9.2 %copy-start.4 = (f32[16,32,128]{2,1,0:T(8,128)S(1)}, f32[16,32,128]{2,1,0:T(8,128)}, u32[]{:S(2)}) copy-start(f32[16,32,128]{2,1,0:T(8,128)} %copy-done.3) | copy-start | bytes 786436
  231.9 9.2 %copy-start.6 = (f32[16,32,128]{2,1,0:T(8,128)S(1)}, f32[16,32,128]{2,1,0:T(8,128)}, u32[]{:S(2)}) copy-start(f32[16,32,128]{2,1,0:T(8,128)} %copy-done.5) | copy-start | bytes 786436
  243.0 0.7 copy-start.11
  261.9 16.8 %all-to-all-start.7 = ((f32[64,16,1,128]{3,1,2,0:T(8,128)}), f32[64,16,1,128]{3,1,2,0:T(8,128)S(1)}, u32[]{:S(2)}, u32[]{:S(2)}) async-start(f32[64,16,1,128]{3,1,2,0:T(8,128)} %copy.90), calls=%async_computation.7 | async-start | bytes 1048576 | tf_op jit(solution)/shard_map/all_to_all | solution.py:143
  278.7 17.5 %all-to-all-start.8 = ((f32[64,16,1,128]{3,1,2,0:T(8,128)}), f32[64,16,1,128]{3,1,2,0:T(8,128)}, u32[]{:S(2)}, u32[]{:S(2)}) async-start(f32[64,16,1,128]{3,1,2,0:T(8,128)} %copy.93), calls=%async_computation.8 | async-start | bytes 1048576 | tf_op jit(solution)/shard_map/all_to_all | solution.py:146
  283.8 0.8 copy-start.1
  298.3 1.0 copy-start.2
  308.8 1.2 copy-start.10
  316.5 16.8 %all-to-all-start.9 = ((f32[2,16,32,128]{3,0,1,2:T(2,128)}), f32[2,16,32,128]{3,0,1,2:T(2,128)S(1)}, u32[]{:S(2)}, u32[]{:S(2)}) async-start(f32[2,16,32,128]{3,0,1,2:T(2,128)} %copy.98), calls=%async_computation.9 | async-start | bytes 1048576 | tf_op jit(solution)/shard_map/all_to_all | solution.py:167
  333.3 16.8 %all-to-all-start.10 = ((f32[2,16,32,128]{3,0,1,2:T(2,128)}), f32[2,16,32,128]{3,0,1,2:T(2,128)S(1)}, u32[]{:S(2)}, u32[]{:S(2)}) async-start(f32[2,16,32,128]{3,0,1,2:T(2,128)} %copy.100), calls=%async_computation.10 | async-start | bytes 1048576 | tf_op jit(solution)/shard_map/all_to_all | solution.py:170
  337.2 171.5 %all-reduce.5.cloned.1.call-start = ((), (), s32[]{:S(2)}) async-start(), calls=%async_computation.12 | async-start | bytes 524288 | tf_op jit(solution)/shard_map/psum | solution.py:250
Sparse Core Ops, SparseCore 0:
  366.7 141.9 all-reduce.4
where the time goes:
time: 526 us; the launch traced here: 519 us
  blocking collectives  226 us (43%)
  waiting for transfers between devices  138 us (26%)
  starting transfers between devices  46.6 us (9%)
  matrix products  43.1 us (8%)
  local copies, waits for them, and re-layouts  30.8 us (6%)
  between operations  17.4 us (3%)
  other arithmetic  16.5 us (3%)
    psum x1, blocking collectives, per_device(): error_sum = lax.psum(jnp.sum(residual * residual), ('chan', 'tm'))  129 us
    unnamed x1, blocking collectives  67.5 us
    all_to_all x2, waiting for transfers between devices, forward_spectrum(): lax.all_to_all(twist_real.reshape(shape_four), 'tm', split_axis=0, concat...  31.6 us
    all_to_all x2, waiting for transfers between devices, forward_spectrum(): lax.all_to_all(twist_imag.reshape(shape_four), 'tm', split_axis=0, concat...  26.7 us
    all_to_all x2, waiting for transfers between devices, inverse_real(): lax.all_to_all(wave_imag.reshape(shape_four), 'tm', split_axis=2, concat_...  24.4 us
    dot_general x16, matrix products, matmul(): jnp.dot(first_op, second_op, precision=highest, preferred_element_type=jn...  22.8 us
    all_to_all x2, waiting for transfers between devices, inverse_real(): lax.all_to_all(wave_real.reshape(shape_four), 'tm', split_axis=2, concat_...  20.5 us
    all_to_all x1, blocking collectives, forward_spectrum(): lax.all_to_all(values.reshape(count_rows, shards, slice_len), 'tm', split...  15.5 us
  transfers between devices with their start and end apart: 12, of which 12 were waited for; matrix products, arithmetic and copies ran while one was open for 3% of the time, Pallas kernels for 0%

commit v1 on v0

v1 whole, which is shorter than its diff:
```python
import math

import jax
import jax.numpy as jnp
import numpy as np
from jax import lax
from jax.experimental import pallas as pl
from jax.experimental.pallas import tpu as pltpu
from jax.sharding import PartitionSpec as P

CHANNELS = 256
LENGTH = 131072
N1, N2 = 512, 256
HALF = 256
SHARDS = 32
SEGS = 32
LANES = 128
var_floor = 1.0
MESH = pl.DeviceIdType.MESH
f32, bf16 = jnp.float32, jnp.bfloat16


def split_table(table):
    high = table.astype(np.float32).astype(bf16)
    low = (table - np.asarray(high).astype(np.float64)).astype(np.float32).astype(bf16)
    return np.asarray(high), np.asarray(low)


def make_tables():
    n1, n2 = np.arange(N1), np.arange(N2)
    k1 = np.arange(HALF)
    angle = 2 * math.pi * ((np.outer(4 * k1 + 1, n1) % (4 * N1)) / (4 * N1))
    outer = np.concatenate([np.cos(angle), -np.sin(angle)], axis=0)
    angle = 2 * math.pi * ((np.outer(n2, n2) % N2) / N2)
    inner = np.concatenate([np.cos(angle), np.sin(angle)], axis=1)
    angle = 2 * math.pi * (np.outer(4 * k1 + 1, n2) / (4 * LENGTH))
    twist = np.stack([np.cos(angle), -np.sin(angle)]).astype(np.float32)
    angle = math.pi * n2 / 256
    lane = np.zeros((8, N2), np.float32)
    lane[0], lane[1] = np.cos(angle), -np.sin(angle)
    return split_table(outer), split_table(outer.T), split_table(inner), twist, lane


def high_low(value):
    high = value.astype(bf16)
    return high, (value - high.astype(f32)).astype(bf16)


def three_way(value):
    high = value.astype(bf16)
    rest = value - high.astype(f32)
    middle = rest.astype(bf16)
    return high, middle, (rest - middle.astype(f32)).astype(bf16)


def dot(first, second):
    return jnp.dot(first, second, preferred_element_type=f32)


def kernel(
    signal, filters, scale_in, shift_in,
    outer_h, outer_l, outer_th, outer_tl, inner_h, inner_l, twist_hbm, lane_ref,
    pred_out, grad_out, loss_out,
    signal_send, filter_send, gate_send, gate_got,
    xbuf, fbuf, pbuf, ybuf, ygot, cbuf, cgot, rsbuf, rsum, prbuf, gbuf,
    loss_own, loss_mid, loss_sum, loss_all,
    outer_k, outer_tk, inner_k, twist,
    triple_x, triple_q, tri_up, tri_low, totals,
    spread_s, normed_s, gating_s, stack, left, spec_x, spec_f,
    table_sem, send_sem, recv_sem,
):
    group, at = lax.axis_index("chan"), lax.axis_index("tm")
    plane, core = group // 2, group % 2
    parity, owned = at % 2, at // 2
    filter_row = 2 * plane + parity
    partner = 2 * plane + 1 - core
    own_half = pl.multiple_of(core * 16, 16)

    def fetch(source, target, number):
        return pltpu.make_async_copy(source, target, table_sem.at[number])

    tables = [
        (outer_h, outer_k.at[:, pl.ds(0, N1)]), (outer_h, outer_k.at[:, pl.ds(N1, N1)]),
        (outer_l, outer_k.at[:, pl.ds(2 * N1, N1)]),
        (outer_th, outer_tk.at[:, pl.ds(0, N1)]), (outer_th, outer_tk.at[:, pl.ds(N1, N1)]),
        (outer_tl, outer_tk.at[:, pl.ds(2 * N1, N1)]),
        (inner_h, inner_k.at[pl.ds(0, N2)]), (inner_h, inner_k.at[pl.ds(N2, N2)]),
        (inner_l, inner_k.at[pl.ds(2 * N2, N2)]),
        (twist_hbm, twist),
    ]

    def remote(source, target, number, chan, tm):
        return pltpu.make_async_remote_copy(
            src_ref=source, dst_ref=target, send_sem=send_sem.at[number], recv_sem=recv_sem.at[number],
            device_id=(chan, tm), device_id_type=MESH,
        )

    def deliver(source, target, number, chan, tm):
        here = jnp.logical_and(chan == group, tm == at)

        @pl.when(jnp.logical_not(here))
        def _():
            remote(source, target, number, chan, tm).start()

        @pl.when(here)
        def _():
            pltpu.make_async_copy(source, target, recv_sem.at[number]).start()

    def arrived(target, number):
        pltpu.make_async_copy(target, target, recv_sem.at[number]).wait()

    def sent(source, number):
        pltpu.make_async_copy(source, source, send_sem.at[number]).wait()

    for seg in range(SEGS):
        signal_send[pl.ds(seg, 16, stride=SEGS), :] = signal[:, seg * LANES : (seg + 1) * LANES]
    signal_rows = signal_send.reshape(16, SEGS, LANES)

    def send_signal(step, carry):
        which = (step + at) % 32
        row, half = which // 2, which % 2
        part = pl.ds(pl.multiple_of(half * 16, 16), 16)
        deliver(
            signal_rows.at[row, part], xbuf.at[at, part], 0,
            2 * (row // 2) + half, 2 * group + row % 2,
        )
        return carry

    lax.fori_loop(0, 32, send_signal, 0)

    gate_send[0:1, 0:16] = scale_in[...]
    gate_send[1:2, 0:16] = shift_in[...]

    @pl.when(owned == group)
    def _():
        def send_gate(step, carry):
            deliver(gate_send, gate_got, 1, (group + step) % 16, at)
            return carry

        lax.fori_loop(0, 16, send_gate, 0)

    for seg in range(SEGS):
        filter_send[pl.ds(seg, 16, stride=SEGS), :] = filters[:, seg * LANES : (seg + 1) * LANES]
    filter_rows = filter_send.reshape(16, SEGS, LANES)

    def send_filter(step, carry):
        to = (step + at) % 32
        deliver(
            filter_rows.at[2 * plane + to % 2, pl.ds(own_half, 16)],
            fbuf.at[at, pl.ds(own_half, 16)], 2, group, to,
        )
        return carry

    lax.fori_loop(0, 32, send_filter, 0)

    for number, (source, target) in enumerate(tables):
        fetch(source, target, number).start()

    row_up = lax.broadcasted_iota(jnp.int32, (N2, N2), 0)
    col_up = lax.broadcasted_iota(jnp.int32, (N2, N2), 1)
    tri_up[...] = jnp.where(row_up <= col_up, 1.0, 0.0).astype(bf16)
    row_low = lax.broadcasted_iota(jnp.int32, (N1, N1), 0)
    col_low = lax.broadcasted_iota(jnp.int32, (N1, N1), 1)
    tri_low[...] = jnp.where(col_low < row_low, 1.0, 0.0).astype(bf16)

    for number, (source, target) in enumerate(tables):
        fetch(source, target, number).wait()
    core_f = core.astype(f32)
    lane_r = 1.0 + core_f * (lane_ref[0:1, :] - 1.0)
    lane_i = core_f * lane_ref[1:2, :]
    base_r, base_i = twist[0], twist[1]
    twist[0] = base_r * lane_r - base_i * lane_i
    twist[1] = base_r * lane_i + base_i * lane_r

    rows_here = lax.broadcasted_iota(jnp.int32, (32, 1), 0)
    flip = 1.0 - 2.0 * core_f * (rows_here % 2).astype(f32)
    all_rows = lax.broadcasted_iota(jnp.int32, (N1, 1), 0)
    flip_all = 1.0 - 2.0 * core_f * (all_rows % 2).astype(f32)

    x_lin = xbuf.reshape(SHARDS * SEGS, LANES)
    f_lin = fbuf.reshape(SHARDS * SEGS, LANES)
    p_lin = pbuf.reshape(SHARDS * SEGS, LANES)
    c_lin = cbuf.reshape(SHARDS * SEGS, LANES)

    def pair_rows(ref, q):
        base = pl.multiple_of(q * 64, 64)
        return jnp.concatenate(
            [ref[pl.ds(base, 32, stride=2), :], ref[pl.ds(base + 1, 32, stride=2), :]], axis=1
        )

    def put_pairs(ref, q, value):
        base = pl.multiple_of(q * 64, 64)
        ref[pl.ds(base, 32, stride=2), :] = value[:, :LANES]
        ref[pl.ds(base + 1, 32, stride=2), :] = value[:, LANES:]

    def rows(q, offset=0):
        return pl.ds(pl.multiple_of(q * 32 + offset, 32), 32)

    def fill_stack(q, value):
        high, low = high_low(value * flip)
        stack[rows(q), :] = high
        stack[rows(q, N1), :] = low
        stack[rows(q, 2 * N1), :] = high

    def fill_left(real, imag):
        for part, value in enumerate((real, imag)):
            high, low = high_low(value)
            place = slice(part * HALF, (part + 1) * HALF)
            left[place, 0:N2] = high
            left[place, N2 : 2 * N2] = low
            left[place, 2 * N2 : 3 * N2] = high

    def forward():
        first = dot(outer_k[...], stack[...])
        first_r, first_i = first[:HALF], first[HALF:]
        fill_left(first_r * twist[0] - first_i * twist[1], first_r * twist[1] + first_i * twist[0])
        quads = dot(left[...], inner_k[...])
        return quads[:HALF, :N2] + quads[HALF:, N2:], quads[HALF:, :N2] - quads[:HALF, N2:]

    def inverse(real, imag):
        fill_left(real, imag)
        quads = dot(left[...], inner_k[...])
        mid_r = quads[:HALF, :N2] - quads[HALF:, N2:]
        mid_i = quads[HALF:, :N2] + quads[:HALF, N2:]
        high, low = high_low(mid_r * twist[0] + mid_i * twist[1])
        stack[0:HALF, :] = high
        stack[N1 : N1 + HALF, :] = low
        stack[2 * N1 : 2 * N1 + HALF, :] = high
        high, low = high_low(mid_i * twist[0] - mid_r * twist[1])
        stack[HALF:N1, :] = high
        stack[N1 + HALF : 2 * N1, :] = low
        stack[2 * N1 + HALF : 3 * N1, :] = high
        return dot(outer_tk[...], stack[...]) * flip_all

    def swap(source, target, number):
        copy = remote(source, target, number, partner, at)
        copy.start()
        return copy

    arrived(xbuf.at[:, pl.ds(own_half, 16)], 0)
    copy = swap(xbuf.at[:, pl.ds(own_half, 16)], xbuf.at[:, pl.ds(own_half, 16)], 3)
    copy.wait()

    def split_rows(q, carry):
        value = pair_rows(x_lin, q)
        for part, piece in enumerate(three_way(value)):
            triple_x[rows(q, part * N1), :] = piece
        for part, piece in enumerate(three_way(value * value)):
            triple_q[rows(q, part * N1), :] = piece
        return carry

    lax.fori_loop(0, 16, split_rows, 0)
    sums = dot(triple_x[...], tri_up[...])
    normed_s[...] = sums[:N1] + sums[N1 : 2 * N1] + sums[2 * N1 :]
    sums = dot(triple_q[...], tri_up[...])
    spread_s[...] = sums[:N1] + sums[N1 : 2 * N1] + sums[2 * N1 :]
    row_sums = jnp.concatenate(
        [
            jnp.broadcast_to(normed_s[:, N2 - 1 : N2], (N1, LANES)),
            jnp.broadcast_to(spread_s[:, N2 - 1 : N2], (N1, LANES)),
        ],
        axis=1,
    )
    carried = dot(tri_low[...], jnp.concatenate(three_way(row_sums), axis=1))
    totals[...] = carried[:, :N2] + carried[:, N2 : 2 * N2] + carried[:, 2 * N2 :]

    arrived(gate_got, 1)
    pick = lax.broadcasted_iota(jnp.int32, (1, LANES), 1) == filter_row
    gate_gain = jnp.sum(jnp.where(pick, gate_got[0:1, :], 0.0), axis=1, keepdims=True)
    gate_bias = jnp.sum(jnp.where(pick, gate_got[1:2, :], 0.0), axis=1, keepdims=True)

    lane_index = lax.broadcasted_iota(jnp.int32, (32, N2), 1)
    row_index = lax.broadcasted_iota(jnp.int32, (32, N2), 0)

    def normalize(q, carry):
        value = pair_rows(x_lin, q)
        before = totals[rows(q), :]
        first = normed_s[rows(q), :] + jnp.concatenate([before[:, :LANES]] * 2, axis=1)
        second = spread_s[rows(q), :] + jnp.concatenate([before[:, LANES:]] * 2, axis=1)
        counts = ((q * 32 + row_index) * N2 + lane_index + 1).astype(f32)
        mean = first / counts
        variance = second / counts - mean * mean
        spread = jnp.sqrt(jnp.maximum(variance, var_floor))
        normed = (value - mean) / spread
        gating_s[rows(q), :] = 1.0 / (1.0 + jnp.exp(-(gate_gain * normed + gate_bias)))
        spread_s[rows(q), :] = spread
        fill_stack(q, normed)
        return carry

    lax.fori_loop(0, 16, normalize, 0)
    real, imag = forward()
    spec_x[0], spec_x[1] = real, imag

    arrived(fbuf.at[:, pl.ds(own_half, 16)], 2)
    copy = swap(fbuf.at[:, pl.ds(own_half, 16)], fbuf.at[:, pl.ds(own_half, 16)], 4)
    copy.wait()

    def take_filter(q, carry):
        fill_stack(q, pair_rows(f_lin, q))
        return carry

    lax.fori_loop(0, 16, take_filter, 0)
    real, imag = forward()
    factor = 1.0 / math.sqrt(LENGTH) / LENGTH
    real, imag = real * factor, imag * factor
    ybuf[...] = inverse(
        spec_x[0] * real - spec_x[1] * imag, spec_x[0] * imag + spec_x[1] * real
    )
    copy = swap(ybuf, ygot, 5)
    copy.wait()

    loss_own[...] = jnp.zeros((8, LANES), f32)

    def predict(q, carry):
        value = pair_rows(x_lin, q)
        opening = x_lin[pl.ds(pl.multiple_of(q * 64, 64), 32, stride=2), :][:, 0:1]
        after = jnp.minimum(q * 64 + 64, SHARDS * SEGS - 8)
        following = x_lin[pl.ds(pl.multiple_of(after, 8), 8), :][0:1, 0:1]
        edge = jnp.concatenate([opening[1:], following], axis=0)
        target = jnp.concatenate([value[:, 1:], edge], axis=1)
        weight = spread_s[rows(q), :] * gating_s[rows(q), :]
        own = ybuf[rows(q), :]
        other = ygot[rows(q), :]
        low_part = jnp.where(core == 0, own, other)
        high_part = jnp.where(core == 0, other, own)
        predicted = value + weight * (low_part + high_part)
        put_pairs(p_lin, q, predicted)
        step_index = (q * 32 + row_index) * N2 + lane_index
        residual = jnp.where(step_index < LENGTH - 1, predicted - target, 0.0)
        squares = residual * residual
        squares = squares[:, :LANES] + squares[:, LANES:]
        loss_own[...] += (squares[0:8] + squares[8:16]) + (squares[16:24] + squares[24:32])
        fill_stack(q, (2.0 / CHANNELS) * residual * weight)
        return carry

    lax.fori_loop(0, 16, predict, 0)

    def send_predicted(step, carry):
        to = (step + at) % 32
        deliver(
            pbuf.at[to, pl.ds(own_half, 16)], prbuf.at[filter_row, pl.ds(own_half, 16)], 6, owned, to
        )
        return carry

    lax.fori_loop(0, 32, send_predicted, 0)

    def send_loss(step, carry):
        deliver(loss_own, loss_mid.at[owned], 7, group, 2 * ((owned + step) % 16) + parity)
        return carry

    lax.fori_loop(0, 16, send_loss, 0)

    real, imag = forward()
    across_r = (real * spec_x[0] + imag * spec_x[1]) * factor
    across_i = (imag * spec_x[0] - real * spec_x[1]) * factor
    ybuf[...] = inverse(across_r, across_i)
    copy = swap(ybuf, cgot, 8)

    arrived(loss_mid, 7)
    loss_sum[...] = jnp.sum(loss_mid[...], axis=0)
    block = 2 * owned + core

    def send_loss_sum(step, carry):
        deliver(loss_sum, loss_all.at[filter_row], 9, (group + step) % 16, block)
        return carry

    lax.fori_loop(0, 16, send_loss_sum, 0)
    copy.wait()

    def add_halves(q, carry):
        put_pairs(c_lin, q, ybuf[rows(q), :] + cgot[rows(q), :])
        return carry

    lax.fori_loop(0, 16, add_halves, 0)

    def send_grad(step, carry):
        to = (owned + step) % 16
        deliver(cbuf.at[2 * to + core], rsbuf.at[owned], 10, group, 2 * to + parity)
        return carry

    lax.fori_loop(0, 16, send_grad, 0)
    arrived(rsbuf, 10)
    rsum[...] = jnp.sum(rsbuf[...], axis=0)

    def send_total(step, carry):
        deliver(rsum, gbuf.at[filter_row], 11, (group + step) % 16, block)
        return carry

    lax.fori_loop(0, 16, send_total, 0)

    arrived(prbuf, 6)
    pr_lin = prbuf.reshape(16 * SEGS, LANES)
    for seg in range(SEGS):
        pred_out[:, seg * LANES : (seg + 1) * LANES] = pr_lin[pl.ds(seg, 16, stride=SEGS), :]

    arrived(loss_all, 9)
    everything = jnp.sum(jnp.sum(loss_all[...], axis=0), keepdims=True)
    loss_out[...] = everything / (CHANNELS * (LENGTH - 1))

    arrived(gbuf, 11)
    g_lin = gbuf.reshape(16 * SEGS, LANES)
    for seg in range(SEGS):
        grad_out[:, seg * LANES : (seg + 1) * LANES] = g_lin[pl.ds(seg, 16, stride=SEGS), :]

    def drain(here, whole, less, number):
        @pl.when(here)
        def _():
            sent(less, number)

        @pl.when(jnp.logical_not(here))
        def _():
            sent(whole, number)

    own_row = owned == group
    drain(own_row, xbuf.at[pl.ds(0, 32), pl.ds(0, 16)], xbuf.at[pl.ds(0, 31), pl.ds(0, 16)], 0)

    @pl.when(own_row)
    def _():
        sent(loss_mid.at[pl.ds(0, 15)], 1)

    sent(xbuf.at[pl.ds(0, 31), pl.ds(0, 16)], 2)
    drain(own_row, xbuf.at[pl.ds(0, 32), pl.ds(0, 16)], xbuf.at[pl.ds(0, 31), pl.ds(0, 16)], 6)
    sent(loss_mid.at[pl.ds(0, 15)], 7)
    drain(core == parity, loss_mid.at[pl.ds(0, 16)], loss_mid.at[pl.ds(0, 15)], 9)
    sent(rsbuf.at[pl.ds(0, 15)], 10)
    drain(core == parity, rsbuf.at[pl.ds(0, 16)], rsbuf.at[pl.ds(0, 15)], 11)


def per_device(signal, filters, gate_scale, gate_shift):
    (outer_h, outer_l), (outer_th, outer_tl), (inner_h, inner_l), twist, lane = make_tables()
    vmem = pl.BlockSpec(memory_space=pltpu.VMEM)
    anywhere = pl.BlockSpec(memory_space=pl.ANY)

    def space(*shape, kind=f32):
        return pltpu.VMEM(shape, kind)

    predicted, grad, loss = pl.pallas_call(
        kernel,
        out_shape=(
            jax.ShapeDtypeStruct((16, 4096), f32),
            jax.ShapeDtypeStruct((16, 4096), f32),
            jax.ShapeDtypeStruct((1, 1), f32),
        ),
        in_specs=[vmem] * 4 + [anywhere] * 7 + [vmem],
        out_specs=(vmem, vmem, vmem),
        scratch_shapes=[
            space(512, LANES), space(512, LANES), space(8, LANES), space(8, LANES),
            space(SHARDS, SEGS, LANES), space(SHARDS, SEGS, LANES), space(SHARDS, SEGS, LANES),
            space(N1, N2), space(N1, N2), space(SHARDS, SEGS, LANES), space(N1, N2),
            space(16, SEGS, LANES), space(SEGS, LANES), space(16, SEGS, LANES), space(16, SEGS, LANES),
            space(8, LANES), space(16, 8, LANES), space(8, LANES), space(16, 8, LANES),
            space(N1, 3 * N1, kind=bf16), space(N1, 3 * N1, kind=bf16), space(3 * N2, 2 * N2, kind=bf16),
            space(2, HALF, N2),
            space(3 * N1, N2, kind=bf16), space(3 * N1, N2, kind=bf16),
            space(N2, N2, kind=bf16), space(N1, N1, kind=bf16), space(N1, N2),
            space(N1, N2), space(N1, N2), space(N1, N2), space(3 * N1, N2, kind=bf16),
            space(N1, 3 * N2, kind=bf16), space(2, HALF, N2), space(2, HALF, N2),
            pltpu.SemaphoreType.DMA((10,)), pltpu.SemaphoreType.DMA((12,)), pltpu.SemaphoreType.DMA((12,)),
        ],
        compiler_params=pltpu.CompilerParams(has_side_effects=True),
    )(
        signal, filters, gate_scale.reshape(1, 16), gate_shift.reshape(1, 16),
        outer_h, outer_l, outer_th, outer_tl, inner_h, inner_l, twist, lane,
    )
    return (predicted, grad, loss.reshape(()))


def solution(mesh):
    return jax.shard_map(
        per_device,
        mesh=mesh,
        in_specs=(P("chan", "tm"), P(None, "tm"), P("chan"), P("chan")),
        out_specs=(P("chan", "tm"), P(None, "tm"), P()),
        check_vma=False,
    )
```

time: 526 us -> 105 us (0.20); the launches traced: 519 us -> 105 us
  blocking collectives: 226 us -> 0 us
  waiting for transfers between devices: 138 us -> 0 us
  Pallas kernels: 0 us -> 100 us
  starting transfers between devices: 46.6 us -> 0 us
  matrix products: 43.1 us -> 0 us
  local copies, waits for them, and re-layouts: 30.8 us -> 2.42 us
  other arithmetic: 16.5 us -> 0 us
  between operations: 17.4 us -> 2.41 us
    psum x1 -> x0, blocking collectives: 129 us -> none  [per_device(): error_sum = lax.psum(jnp.sum(residual * residual), ('chan', 'tm'))]
    all_to_all x10 -> x0, waiting for transfers between devices: 122 us -> none  [the longest x2 31.6 us: forward_spectrum(): lax.all_to_all(twist_real.reshape(shape_four), 'tm', split_axis=0, concat...]
    pallas_call x0 -> x1, Pallas kernels: none -> 100 us  [per_device(): pl.pallas_call(kernel, out_shape=(jax.ShapeDtypeStruct((16, 4096), f32),...]
    unnamed x1 -> x0, blocking collectives: 67.5 us -> none
    all_to_all x10 -> x0, starting transfers between devices: 45.2 us -> none  [the longest x2 9.23 us: inverse_real(): lax.all_to_all(wave_real.reshape(shape_four), 'tm', split_axis=2, concat_...]
    dot_general x40 -> x0, matrix products: 43.1 us -> none  [the longest x16 22.8 us: matmul(): jnp.dot(first_op, second_op, precision=highest, preferred_element_type=jn...]
    all_to_all x2 -> x0, blocking collectives: 29.6 us -> none  [the longest x1 15.5 us: forward_spectrum(): lax.all_to_all(values.reshape(count_rows, shards, slice_len), 'tm', split...]
    psum x1 -> x0, waiting for transfers between devices: 12.8 us -> none  [per_device(): grad_filter = lax.psum(local_grad * tap_scale, 'chan')]
  transfers between devices with their start and end apart: 12 -> 0, of which waited for: 12 -> 0; matrix products, arithmetic and copies ran while one was open for 3% -> 0% of each run, Pallas kernels for 0% -> 0%
where the time goes in v1:
time: 105 us
  Pallas kernels  100 us (95%)
  local copies, waits for them, and re-layouts  2.42 us (2%)
  between operations  2.41 us (2%)
    pallas_call x1, Pallas kernels, per_device(): pl.pallas_call(kernel, out_shape=(jax.ShapeDtypeStruct((16, 4096), f32),...  100 us
    unnamed x4, local copies, waits for them, and re-layouts  2.42 us

profile of v1, /device:TPU:1, one launch (start us, length us, event | category | flops | bytes accessed | tf_op | source)
XLA Modules:
  0.0 105.1 jit_solution(10910649573347495166)
XLA Ops:
  0.6 100.2 %shard_map.139 = (f32[16,4096]{1,0:T(8,128)}, f32[16,4096]{1,0:T(8,128)}, f32[1,1]{1,0:T(1,128)}) custom-call(f32[16,4096]{1,0:T(8,128)} %signal.1, f32[16,4096]{1,0:T(8,128)} %filters.1, f32[1,16]{1,0:T(1,128)} %bitcast.3, f32[1,16]{1,0:T(1,128)} %bitcast.4, bf16[512,512]{1,0:T(8,128)(2,1)} %constant.16.clone.outer_h, ...), custom_call_target="tpu_custom_call" | custom-call | tf_op jit(solution)/shard_map/pallas_call | solution.py:437
  100.9 0.0 copy-start
  100.9 1.7 %copy.18 = f32[16,4096]{1,0:T(8,128)} copy(f32[16,4096]{1,0:T(8,128)} %get-tuple-element.12) | data formatting | bytes 524288
  102.6 0.0 copy-done
  102.6 0.7 copy.19
Async XLA Ops:
  100.9 1.7 %copy-start = (f32[16,4096]{1,0:T(8,128)S(1)}, f32[16,4096]{1,0:T(8,128)}, u32[]{:S(2)}) copy-start(f32[16,4096]{1,0:T(8,128)} %get-tuple-element.13) | copy-start | bytes 786436

commit v2 on v1

--- a/solution.py
+++ b/solution.py
@@ -62,19 +62,41 @@
     outer_h, outer_l, outer_th, outer_tl, inner_h, inner_l, twist_hbm, lane_ref,
     pred_out, grad_out, loss_out,
     signal_send, filter_send, gate_send, gate_got,
-    xbuf, fbuf, pbuf, ybuf, ygot, cbuf, cgot, rsbuf, rsum, prbuf, gbuf,
-    loss_own, loss_mid, loss_sum, loss_all,
+    xbuf, fbuf, pbuf, ybuf, ygot, cbuf, cgot, csum, along_y, along_sum, across, across_sum,
+    loss_acc, loss_own, loss_mid, loss_sum, loss_all,
     outer_k, outer_tk, inner_k, twist,
     triple_x, triple_q, tri_up, tri_low, totals,
-    spread_s, normed_s, gating_s, stack, left, spec_x, spec_f,
+    spread_s, normed_s, gating_s, stack, left, spec_x,
     table_sem, send_sem, recv_sem,
 ):
     group, at = lax.axis_index("chan"), lax.axis_index("tm")
     plane, core = group // 2, group % 2
-    parity, owned = at % 2, at // 2
-    filter_row = 2 * plane + parity
+    owner_core, owner_row = at % 2, at // 2
     partner = 2 * plane + 1 - core
-    own_half = pl.multiple_of(core * 16, 16)
+    own_half = pl.ds(pl.multiple_of(core * 16, 16), 16)
+    own_piece = pl.ds(pl.multiple_of((plane // 2) * 8, 8), 8)
+    on_plane = plane % 2
+    active = at % 2 == on_plane
+    row_odd = owner_row % 2
+
+    barrier = pltpu.get_barrier_semaphore()
+
+    def greet(step, carry):
+        other = (core * SHARDS + at + step) % (2 * SHARDS)
+        pl.semaphore_signal(
+            barrier, inc=1, device_id=(2 * plane + other // SHARDS, other % SHARDS), device_id_type=MESH
+        )
+        return carry
+
+    lax.fori_loop(1, 2 * SHARDS, greet, 0)
+
+    def greet_planes(step, carry):
+        pl.semaphore_signal(
+            barrier, inc=1, device_id=(2 * ((plane + step) % 8) + core, at), device_id_type=MESH
+        )
+        return carry
+
+    lax.fori_loop(1, 8, greet_planes, 0)
 
     def fetch(source, target, number):
         return pltpu.make_async_copy(source, target, table_sem.at[number])
@@ -88,6 +110,8 @@
         (inner_l, inner_k.at[pl.ds(2 * N2, N2)]),
         (twist_hbm, twist),
     ]
+    for number, (source, target) in enumerate(tables):
+        fetch(source, target, number).start()
 
     def remote(source, target, number, chan, tm):
         return pltpu.make_async_remote_copy(
@@ -112,56 +136,52 @@
     def sent(source, number):
         pltpu.make_async_copy(source, source, send_sem.at[number]).wait()
 
+    def swap(source, target, number):
+        copy = remote(source, target, number, partner, at)
+        copy.start()
+        return copy
+
     for seg in range(SEGS):
         signal_send[pl.ds(seg, 16, stride=SEGS), :] = signal[:, seg * LANES : (seg + 1) * LANES]
     signal_rows = signal_send.reshape(16, SEGS, LANES)
-
-    def send_signal(step, carry):
-        which = (step + at) % 32
-        row, half = which // 2, which % 2
-        part = pl.ds(pl.multiple_of(half * 16, 16), 16)
-        deliver(
-            signal_rows.at[row, part], xbuf.at[at, part], 0,
-            2 * (row // 2) + half, 2 * group + row % 2,
-        )
-        return carry
-
-    lax.fori_loop(0, 32, send_signal, 0)
-
+    gate_send[...] = jnp.zeros((8, LANES), f32)
     gate_send[0:1, 0:16] = scale_in[...]
     gate_send[1:2, 0:16] = shift_in[...]
-
-    @pl.when(owned == group)
-    def _():
-        def send_gate(step, carry):
-            deliver(gate_send, gate_got, 1, (group + step) % 16, at)
-            return carry
-
-        lax.fori_loop(0, 16, send_gate, 0)
-
     for seg in range(SEGS):
         filter_send[pl.ds(seg, 16, stride=SEGS), :] = filters[:, seg * LANES : (seg + 1) * LANES]
     filter_rows = filter_send.reshape(16, SEGS, LANES)
-
-    def send_filter(step, carry):
-        to = (step + at) % 32
-        deliver(
-            filter_rows.at[2 * plane + to % 2, pl.ds(own_half, 16)],
-            fbuf.at[at, pl.ds(own_half, 16)], 2, group, to,
-        )
-        return carry
-
-    lax.fori_loop(0, 32, send_filter, 0)
-
-    for number, (source, target) in enumerate(tables):
-        fetch(source, target, number).start()
-
     row_up = lax.broadcasted_iota(jnp.int32, (N2, N2), 0)
     col_up = lax.broadcasted_iota(jnp.int32, (N2, N2), 1)
     tri_up[...] = jnp.where(row_up <= col_up, 1.0, 0.0).astype(bf16)
     row_low = lax.broadcasted_iota(jnp.int32, (N1, N1), 0)
     col_low = lax.broadcasted_iota(jnp.int32, (N1, N1), 1)
     tri_low[...] = jnp.where(col_low < row_low, 1.0, 0.0).astype(bf16)
+
+    pl.semaphore_wait(barrier, 2 * SHARDS - 1 + 7)
+
+    def send_signal(step, carry):
+        which = (step + at) % 32
+        row, half = which // 2, which % 2
+        part = pl.ds(pl.multiple_of(half * 16, 16), 16)
+        deliver(
+            signal_rows.at[row, part], xbuf.at[at, part], 0, 2 * plane + half, 2 * row + core
+        )
+        return carry
+
+    lax.fori_loop(0, 32, send_signal, 0)
+    gates = swap(gate_send, gate_got, 1)
+
+    @pl.when(active)
+    def _():
+        def send_filter(step, carry):
+            row = (step + owner_row) % 16
+            deliver(
+                filter_rows.at[row, own_piece], fbuf.at[at // 4, at % 4, own_piece], 2,
+                2 * plane + row_odd, 2 * row + core,
+            )
+            return carry
+
+        lax.fori_loop(0, 16, send_filter, 0)
 
     for number, (source, target) in enumerate(tables):
         fetch(source, target, number).wait()
@@ -232,13 +252,16 @@
         stack[2 * N1 + HALF : 3 * N1, :] = high
         return dot(outer_tk[...], stack[...]) * flip_all
 
-    def swap(source, target, number):
-        copy = remote(source, target, number, partner, at)
-        copy.start()
-        return copy
-
-    arrived(xbuf.at[:, pl.ds(own_half, 16)], 0)
-    copy = swap(xbuf.at[:, pl.ds(own_half, 16)], xbuf.at[:, pl.ds(own_half, 16)], 3)
+    own_blocks = fbuf.at[:, 2 * core + on_plane, own_piece]
+    arrived(own_blocks, 2)
+
+    def gather_filter(step, carry):
+        remote(own_blocks, own_blocks, 3, 2 * ((plane + step) % 8) + core, at).start()
+        return carry
+
+    lax.fori_loop(1, 8, gather_filter, 0)
+    arrived(xbuf.at[:, own_half], 0)
+    copy = swap(xbuf.at[:, own_half], xbuf.at[:, own_half], 4)
     copy.wait()
 
     def split_rows(q, carry):
@@ -264,10 +287,11 @@
     carried = dot(tri_low[...], jnp.concatenate(three_way(row_sums), axis=1))
     totals[...] = carried[:, :N2] + carried[:, N2 : 2 * N2] + carried[:, 2 * N2 :]
 
-    arrived(gate_got, 1)
-    pick = lax.broadcasted_iota(jnp.int32, (1, LANES), 1) == filter_row
-    gate_gain = jnp.sum(jnp.where(pick, gate_got[0:1, :], 0.0), axis=1, keepdims=True)
-    gate_bias = jnp.sum(jnp.where(pick, gate_got[1:2, :], 0.0), axis=1, keepdims=True)
+    gates.wait()
+    gate_pair = jnp.where(core == owner_core, gate_send[...], gate_got[...])
+    pick = lax.broadcasted_iota(jnp.int32, (1, LANES), 1) == owner_row
+    gate_gain = jnp.sum(jnp.where(pick, gate_pair[0:1, :], 0.0), axis=1, keepdims=True)
+    gate_bias = jnp.sum(jnp.where(pick, gate_pair[1:2, :], 0.0), axis=1, keepdims=True)
 
     lane_index = lax.broadcasted_iota(jnp.int32, (32, N2), 1)
     row_index = lax.broadcasted_iota(jnp.int32, (32, N2), 0)
@@ -288,11 +312,11 @@
         return carry
 
     lax.fori_loop(0, 16, normalize, 0)
+    arrived(xbuf.at[pl.ds(0, 14)], 3)
+    core_blocks = fbuf.at[:, pl.ds(2 * core, 2)]
+    copy = swap(core_blocks, core_blocks, 5)
     real, imag = forward()
     spec_x[0], spec_x[1] = real, imag
-
-    arrived(fbuf.at[:, pl.ds(own_half, 16)], 2)
-    copy = swap(fbuf.at[:, pl.ds(own_half, 16)], fbuf.at[:, pl.ds(own_half, 16)], 4)
     copy.wait()
 
     def take_filter(q, carry):
@@ -306,10 +330,10 @@
     ybuf[...] = inverse(
         spec_x[0] * real - spec_x[1] * imag, spec_x[0] * imag + spec_x[1] * real
     )
-    copy = swap(ybuf, ygot, 5)
+    copy = swap(ybuf, ygot, 6)
     copy.wait()
 
-    loss_own[...] = jnp.zeros((8, LANES), f32)
+    loss_acc[...] = jnp.zeros((8, LANES), f32)
 
     def predict(q, carry):
         value = pair_rows(x_lin, q)
@@ -319,17 +343,13 @@
         edge = jnp.concatenate([opening[1:], following], axis=0)
         target = jnp.concatenate([value[:, 1:], edge], axis=1)
         weight = spread_s[rows(q), :] * gating_s[rows(q), :]
-        own = ybuf[rows(q), :]
-        other = ygot[rows(q), :]
-        low_part = jnp.where(core == 0, own, other)
-        high_part = jnp.where(core == 0, other, own)
-        predicted = value + weight * (low_part + high_part)
+        predicted = value + weight * (ybuf[rows(q), :] + ygot[rows(q), :])
         put_pairs(p_lin, q, predicted)
         step_index = (q * 32 + row_index) * N2 + lane_index
         residual = jnp.where(step_index < LENGTH - 1, predicted - target, 0.0)
         squares = residual * residual
         squares = squares[:, :LANES] + squares[:, LANES:]
-        loss_own[...] += (squares[0:8] + squares[8:16]) + (squares[16:24] + squares[24:32])
+        loss_acc[...] += (squares[0:8] + squares[8:16]) + (squares[16:24] + squares[24:32])
         fill_stack(q, (2.0 / CHANNELS) * residual * weight)
         return carry
 
@@ -338,92 +358,105 @@
     def send_predicted(step, carry):
         to = (step + at) % 32
         deliver(
-            pbuf.at[to, pl.ds(own_half, 16)], prbuf.at[filter_row, pl.ds(own_half, 16)], 6, owned, to
+            pbuf.at[to, own_half], pred_out.at[owner_row, own_half], 7, 2 * plane + owner_core, to
         )
         return carry
 
     lax.fori_loop(0, 32, send_predicted, 0)
+    loss_own[...] = jnp.sum(loss_acc[...], axis=0, keepdims=True)
 
     def send_loss(step, carry):
-        deliver(loss_own, loss_mid.at[owned], 7, group, 2 * ((owned + step) % 16) + parity)
-        return carry
-
-    lax.fori_loop(0, 16, send_loss, 0)
+        deliver(loss_own, loss_mid.at[plane], 8, 2 * ((plane + step) % 8) + core, at)
+        return carry
+
+    lax.fori_loop(0, 8, send_loss, 0)
 
     real, imag = forward()
     across_r = (real * spec_x[0] + imag * spec_x[1]) * factor
     across_i = (imag * spec_x[0] - real * spec_x[1]) * factor
-    ybuf[...] = inverse(across_r, across_i)
-    copy = swap(ybuf, cgot, 8)
-
-    arrived(loss_mid, 7)
+    local = inverse(across_r, across_i)
+    c_lin[pl.ds(0, N1, stride=2), :] = local[:, :LANES]
+    c_lin[pl.ds(1, N1, stride=2), :] = local[:, LANES:]
+    copy = swap(cbuf.at[:, pl.ds(2 * (1 - core), 2)], cgot, 9)
+
+    arrived(loss_mid, 8)
     loss_sum[...] = jnp.sum(loss_mid[...], axis=0)
-    block = 2 * owned + core
 
     def send_loss_sum(step, carry):
-        deliver(loss_sum, loss_all.at[filter_row], 9, (group + step) % 16, block)
-        return carry
-
-    lax.fori_loop(0, 16, send_loss_sum, 0)
+        deliver(loss_sum, loss_all.at[at], 10, group, (at + step) % 32)
+        return carry
+
+    lax.fori_loop(0, 32, send_loss_sum, 0)
     copy.wait()
-
-    def add_halves(q, carry):
-        put_pairs(c_lin, q, ybuf[rows(q), :] + cgot[rows(q), :])
-        return carry
-
-    lax.fori_loop(0, 16, add_halves, 0)
-
-    def send_grad(step, carry):
-        to = (owned + step) % 16
-        deliver(cbuf.at[2 * to + core], rsbuf.at[owned], 10, group, 2 * to + parity)
-        return carry
-
-    lax.fori_loop(0, 16, send_grad, 0)
-    arrived(rsbuf, 10)
-    rsum[...] = jnp.sum(rsbuf[...], axis=0)
-
-    def send_total(step, carry):
-        deliver(rsum, gbuf.at[filter_row], 11, (group + step) % 16, block)
-        return carry
-
-    lax.fori_loop(0, 16, send_total, 0)
-
-    arrived(prbuf, 6)
-    pr_lin = prbuf.reshape(16 * SEGS, LANES)
-    for seg in range(SEGS):
-        pred_out[:, seg * LANES : (seg + 1) * LANES] = pr_lin[pl.ds(seg, 16, stride=SEGS), :]
-
-    arrived(loss_all, 9)
+    csum[...] = cbuf[:, pl.ds(2 * core, 2)] + cgot[...]
+
+    def send_along(step, carry):
+        to = (plane + step) % 8
+        piece = pl.ds(pl.multiple_of((to // 2) * 8, 8), 8)
+        deliver(csum.at[:, to % 2, piece], along_y.at[plane], 11, 2 * to + core, at)
+        return carry
+
+    lax.fori_loop(0, 8, send_along, 0)
+    arrived(along_y, 11)
+    along_sum[...] = jnp.sum(along_y[...], axis=0)
+
+    def send_across(step, carry):
+        deliver(
+            along_sum.at[step], across.at[owner_row // 2, owner_core], 12,
+            2 * plane + row_odd, 4 * step + 2 * core + on_plane,
+        )
+        return carry
+
+    lax.fori_loop(0, 8, send_across, 0)
+
+    @pl.when(active)
+    def _():
+        arrived(across, 12)
+        across_sum[...] = across[:, 0] + across[:, 1]
+
+        def send_total(step, carry):
+            deliver(across_sum, grad_out.at[:, core, own_piece], 13, 2 * ((plane + step) % 8) + core, at)
+            return carry
+
+        lax.fori_loop(0, 8, send_total, 0)
+
+    arrived(loss_all, 10)
     everything = jnp.sum(jnp.sum(loss_all[...], axis=0), keepdims=True)
     loss_out[...] = everything / (CHANNELS * (LENGTH - 1))
 
-    arrived(gbuf, 11)
-    g_lin = gbuf.reshape(16 * SEGS, LANES)
-    for seg in range(SEGS):
-        grad_out[:, seg * LANES : (seg + 1) * LANES] = g_lin[pl.ds(seg, 16, stride=SEGS), :]
-
-    def drain(here, whole, less, number):
-        @pl.when(here)
+    arrived(grad_out.at[:, core], 13)
+    copy = swap(grad_out.at[:, core], grad_out.at[:, core], 14)
+
+    def drain(less, whole, part, number):
+        @pl.when(less)
         def _():
-            sent(less, number)
-
-        @pl.when(jnp.logical_not(here))
+            sent(part, number)
+
+        @pl.when(jnp.logical_not(less))
         def _():
             sent(whole, number)
 
-    own_row = owned == group
-    drain(own_row, xbuf.at[pl.ds(0, 32), pl.ds(0, 16)], xbuf.at[pl.ds(0, 31), pl.ds(0, 16)], 0)
-
-    @pl.when(own_row)
+    own_core = owner_core == core
+    drain(own_core, xbuf.at[:, pl.ds(0, 16)], xbuf.at[pl.ds(0, 31), pl.ds(0, 16)], 0)
+
+    @pl.when(active)
     def _():
-        sent(loss_mid.at[pl.ds(0, 15)], 1)
-
-    sent(xbuf.at[pl.ds(0, 31), pl.ds(0, 16)], 2)
-    drain(own_row, xbuf.at[pl.ds(0, 32), pl.ds(0, 16)], xbuf.at[pl.ds(0, 31), pl.ds(0, 16)], 6)
-    sent(loss_mid.at[pl.ds(0, 15)], 7)
-    drain(core == parity, loss_mid.at[pl.ds(0, 16)], loss_mid.at[pl.ds(0, 15)], 9)
-    sent(rsbuf.at[pl.ds(0, 15)], 10)
-    drain(core == parity, rsbuf.at[pl.ds(0, 16)], rsbuf.at[pl.ds(0, 15)], 11)
+        drain(
+            jnp.logical_and(own_core, row_odd == core),
+            xbuf.at[pl.ds(0, 16), pl.ds(0, 8)], xbuf.at[pl.ds(0, 15), pl.ds(0, 8)], 2,
+        )
+        sent(xbuf.at[pl.ds(0, 14)], 13)
+
+    sent(xbuf.at[pl.ds(0, 14)], 3)
+    drain(own_core, xbuf.at[:, pl.ds(0, 16)], xbuf.at[pl.ds(0, 31), pl.ds(0, 16)], 7)
+    sent(loss_mid.at[pl.ds(0, 7)], 8)
+    sent(loss_all.at[pl.ds(0, 31)], 10)
+    sent(xbuf.at[pl.ds(0, 14)], 11)
+    drain(
+        jnp.logical_and(active, row_odd == core), along_sum, along_sum.at[pl.ds(0, 7)], 12
+    )
+    arrived(pred_out, 7)
+    copy.wait()
 
 
 def per_device(signal, filters, gate_scale, gate_shift):
@@ -437,32 +470,33 @@
     predicted, grad, loss = pl.pallas_call(
         kernel,
         out_shape=(
-            jax.ShapeDtypeStruct((16, 4096), f32),
-            jax.ShapeDtypeStruct((16, 4096), f32),
+            jax.ShapeDtypeStruct((16, SEGS, LANES), f32),
+            jax.ShapeDtypeStruct((8, 2, SEGS, LANES), f32),
             jax.ShapeDtypeStruct((1, 1), f32),
         ),
         in_specs=[vmem] * 4 + [anywhere] * 7 + [vmem],
-        out_specs=(vmem, vmem, vmem),
+        out_specs=(anywhere, anywhere, vmem),
         scratch_shapes=[
             space(512, LANES), space(512, LANES), space(8, LANES), space(8, LANES),
-            space(SHARDS, SEGS, LANES), space(SHARDS, SEGS, LANES), space(SHARDS, SEGS, LANES),
-            space(N1, N2), space(N1, N2), space(SHARDS, SEGS, LANES), space(N1, N2),
-            space(16, SEGS, LANES), space(SEGS, LANES), space(16, SEGS, LANES), space(16, SEGS, LANES),
-            space(8, LANES), space(16, 8, LANES), space(8, LANES), space(16, 8, LANES),
+            space(SHARDS, SEGS, LANES), space(8, 4, SEGS, LANES), space(SHARDS, SEGS, LANES),
+            space(N1, N2), space(N1, N2), space(8, 4, SEGS, LANES), space(8, 2, SEGS, LANES),
+            space(8, 2, SEGS, LANES), space(8, 8, 8, LANES), space(8, 8, LANES),
+            space(8, 2, 8, LANES), space(8, 8, LANES),
+            space(8, LANES), space(1, LANES), space(8, 1, LANES), space(1, LANES), space(32, 1, LANES),
             space(N1, 3 * N1, kind=bf16), space(N1, 3 * N1, kind=bf16), space(3 * N2, 2 * N2, kind=bf16),
             space(2, HALF, N2),
             space(3 * N1, N2, kind=bf16), space(3 * N1, N2, kind=bf16),
             space(N2, N2, kind=bf16), space(N1, N1, kind=bf16), space(N1, N2),
             space(N1, N2), space(N1, N2), space(N1, N2), space(3 * N1, N2, kind=bf16),
-            space(N1, 3 * N2, kind=bf16), space(2, HALF, N2), space(2, HALF, N2),
-            pltpu.SemaphoreType.DMA((10,)), pltpu.SemaphoreType.DMA((12,)), pltpu.SemaphoreType.DMA((12,)),
+            space(N1, 3 * N2, kind=bf16), space(2, HALF, N2),
+            pltpu.SemaphoreType.DMA((10,)), pltpu.SemaphoreType.DMA((15,)), pltpu.SemaphoreType.DMA((15,)),
         ],
-        compiler_params=pltpu.CompilerParams(has_side_effects=True),
+        compiler_params=pltpu.CompilerParams(has_side_effects=True, collective_id=1),
     )(
         signal, filters, gate_scale.reshape(1, 16), gate_shift.reshape(1, 16),
         outer_h, outer_l, outer_th, outer_tl, inner_h, inner_l, twist, lane,
     )
-    return (predicted, grad, loss.reshape(()))
+    return (predicted.reshape(16, 4096), grad.reshape(16, 4096), loss.reshape(()))
 
 
 def solution(mesh):

time: 105 us -> 81.2 us (0.77)
  Pallas kernels: 100 us -> 76.5 us
    pallas_call x1, Pallas kernels: 100 us -> 76.5 us  [per_device(): pl.pallas_call(kernel, out_shape=(jax.ShapeDtypeStruct((16, SEGS, LANES),...]
    unnamed x4 -> x0, local copies, waits for them, and re-layouts: 2.42 us -> none
    reshape x0 -> x1, local copies, waits for them, and re-layouts: none -> 2.12 us  [per_device(): grad.reshape(16, 4096)]
where the time goes in v2:
time: 81.2 us; the launch traced here: 81 us
  Pallas kernels  76.5 us (94%)
  between operations  2.4 us (3%)
  local copies, waits for them, and re-layouts  2.12 us (3%)
    pallas_call x1, Pallas kernels, per_device(): pl.pallas_call(kernel, out_shape=(jax.ShapeDtypeStruct((16, SEGS, LANES),...  76.5 us
    reshape x1, local copies, waits for them, and re-layouts, per_device(): grad.reshape(16, 4096)  2.12 us

profile of v2, /device:TPU:1, one launch (start us, length us, event | category | flops | bytes accessed | tf_op | source)
XLA Modules:
  0.0 81.0 jit_solution(11948014608278457384)
XLA Ops:
  0.6 76.5 %shard_map.139 = (f32[16,32,128]{2,1,0:T(8,128)}, f32[8,2,32,128]{3,2,1,0:T(8,128)}, f32[1,1]{1,0:T(1,128)}) custom-call(f32[16,4096]{1,0:T(8,128)} %signal.1, f32[16,4096]{1,0:T(8,128)} %filters.1, f32[1,16]{1,0:T(1,128)} %bitcast.12, f32[1,16]{1,0:T(1,128)} %bitcast.13, bf16[512,512]{1,0:T(8,128)(2,1)} %constant.16.clone.outer_h, ...), custom_call_target="tpu_custom_call" | custom-call | tf_op jit(solution)/shard_map/pallas_call | solution.py:470
  77.1 2.1 %copy_bitcast_fusion = (f32[16,4096]{1,0:T(8,128)}, f32[16,4096]{1,0:T(8,128)}) fusion(f32[2,8,32,128]{3,2,1,0:T(8,128)} %bitcast.11, f32[2,8,32,128]{3,2,1,0:T(8,128)} %bitcast.10), kind=kLoop, calls=%fused_computation | loop fusion | bytes 1048576 | tf_op jit(solution)/shard_map/reshape | solution.py:499

commit v3 on v2

--- a/solution.py
+++ b/solution.py
@@ -17,6 +17,7 @@
 LANES = 128
 var_floor = 1.0
 MESH = pl.DeviceIdType.MESH
+FAR_FIRST = (4, 3, 5, 2, 6, 1, 7, 0)
 f32, bf16 = jnp.float32, jnp.bfloat16
 
 
@@ -72,6 +73,7 @@
     group, at = lax.axis_index("chan"), lax.axis_index("tm")
     plane, core = group // 2, group % 2
     owner_core, owner_row = at % 2, at // 2
+    depth, width = at // 4, at % 4
     partner = 2 * plane + 1 - core
     own_half = pl.ds(pl.multiple_of(core * 16, 16), 16)
     own_piece = pl.ds(pl.multiple_of((plane // 2) * 8, 8), 8)
@@ -153,35 +155,38 @@
     row_up = lax.broadcasted_iota(jnp.int32, (N2, N2), 0)
     col_up = lax.broadcasted_iota(jnp.int32, (N2, N2), 1)
     tri_up[...] = jnp.where(row_up <= col_up, 1.0, 0.0).astype(bf16)
-    row_low = lax.broadcasted_iota(jnp.int32, (N1, N1), 0)
-    col_low = lax.broadcasted_iota(jnp.int32, (N1, N1), 1)
-    tri_low[...] = jnp.where(col_low < row_low, 1.0, 0.0).astype(bf16)
-
+    def rows(q, offset=0):
+        return pl.ds(pl.multiple_of(q * 32 + offset, 32), 32)
+
+    row_low = lax.broadcasted_iota(jnp.int32, (32, N1), 0)
+    col_low = lax.broadcasted_iota(jnp.int32, (32, N1), 1)
+
+    def fill_low(q, carry):
+        tri_low[rows(q), :] = jnp.where(col_low < row_low + q * 32, 1.0, 0.0).astype(bf16)
+        return carry
+
+    lax.fori_loop(0, 16, fill_low, 0)
     pl.semaphore_wait(barrier, 2 * SHARDS - 1 + 7)
-
-    def send_signal(step, carry):
-        which = (step + at) % 32
-        row, half = which // 2, which % 2
-        part = pl.ds(pl.multiple_of(half * 16, 16), 16)
-        deliver(
-            signal_rows.at[row, part], xbuf.at[at, part], 0, 2 * plane + half, 2 * row + core
-        )
-        return carry
-
-    lax.fori_loop(0, 32, send_signal, 0)
-    gates = swap(gate_send, gate_got, 1)
 
     @pl.when(active)
     def _():
-        def send_filter(step, carry):
-            row = (step + owner_row) % 16
-            deliver(
-                filter_rows.at[row, own_piece], fbuf.at[at // 4, at % 4, own_piece], 2,
-                2 * plane + row_odd, 2 * row + core,
-            )
-            return carry
-
-        lax.fori_loop(0, 16, send_filter, 0)
+        for far in FAR_FIRST:
+            for side in (0, 1):
+                row = 2 * ((depth + far) % 8) + side
+                deliver(
+                    filter_rows.at[row, own_piece], fbuf.at[depth, width, own_piece], 2,
+                    2 * plane + row_odd, 2 * row + core,
+                )
+
+    for far in FAR_FIRST:
+        for side in (0, 1):
+            row = 2 * ((depth + far) % 8) + side
+            for half in (0, 1):
+                part = pl.ds(half * 16, 16)
+                deliver(
+                    signal_rows.at[row, part], xbuf.at[at, part], 0, 2 * plane + half, 2 * row + core
+                )
+    gates = swap(gate_send, gate_got, 1)
 
     for number, (source, target) in enumerate(tables):
         fetch(source, target, number).wait()
@@ -194,8 +199,8 @@
 
     rows_here = lax.broadcasted_iota(jnp.int32, (32, 1), 0)
     flip = 1.0 - 2.0 * core_f * (rows_here % 2).astype(f32)
-    all_rows = lax.broadcasted_iota(jnp.int32, (N1, 1), 0)
-    flip_all = 1.0 - 2.0 * core_f * (all_rows % 2).astype(f32)
+    half_rows = lax.broadcasted_iota(jnp.int32, (HALF, 1), 0)
+    flip_half = 1.0 - 2.0 * core_f * (half_rows % 2).astype(f32)
 
     x_lin = xbuf.reshape(SHARDS * SEGS, LANES)
     f_lin = fbuf.reshape(SHARDS * SEGS, LANES)
@@ -212,9 +217,6 @@
         base = pl.multiple_of(q * 64, 64)
         ref[pl.ds(base, 32, stride=2), :] = value[:, :LANES]
         ref[pl.ds(base + 1, 32, stride=2), :] = value[:, LANES:]
-
-    def rows(q, offset=0):
-        return pl.ds(pl.multiple_of(q * 32 + offset, 32), 32)
 
     def fill_stack(q, value):
         high, low = high_low(value * flip)
@@ -237,7 +239,7 @@
         quads = dot(left[...], inner_k[...])
         return quads[:HALF, :N2] + quads[HALF:, N2:], quads[HALF:, :N2] - quads[:HALF, N2:]
 
-    def inverse(real, imag):
+    def inverse(real, imag, take):
         fill_left(real, imag)
         quads = dot(left[...], inner_k[...])
         mid_r = quads[:HALF, :N2] - quads[HALF:, N2:]
@@ -250,16 +252,15 @@
         stack[HALF:N1, :] = high
         stack[N1 + HALF : 2 * N1, :] = low
         stack[2 * N1 + HALF : 3 * N1, :] = high
-        return dot(outer_tk[...], stack[...]) * flip_all
+        for half in (0, 1):
+            place = slice(half * HALF, (half + 1) * HALF)
+            take(half, dot(outer_tk[place, :], stack[...]) * flip_half)
 
     own_blocks = fbuf.at[:, 2 * core + on_plane, own_piece]
     arrived(own_blocks, 2)
 
-    def gather_filter(step, carry):
-        remote(own_blocks, own_blocks, 3, 2 * ((plane + step) % 8) + core, at).start()
-        return carry
-
-    lax.fori_loop(1, 8, gather_filter, 0)
+    for far in FAR_FIRST[:-1]:
+        remote(own_blocks, own_blocks, 3, 2 * ((plane + far) % 8) + core, at).start()
     arrived(xbuf.at[:, own_half], 0)
     copy = swap(xbuf.at[:, own_half], xbuf.at[:, own_half], 4)
     copy.wait()
@@ -327,11 +328,16 @@
     real, imag = forward()
     factor = 1.0 / math.sqrt(LENGTH) / LENGTH
     real, imag = real * factor, imag * factor
-    ybuf[...] = inverse(
-        spec_x[0] * real - spec_x[1] * imag, spec_x[0] * imag + spec_x[1] * real
+    copies = []
+
+    def exchange(half, value):
+        place = pl.ds(half * HALF, HALF)
+        ybuf[place, :] = value
+        copies.append(swap(ybuf.at[place], ygot.at[place], 6 + 9 * half))
+
+    inverse(
+        spec_x[0] * real - spec_x[1] * imag, spec_x[0] * imag + spec_x[1] * real, exchange
     )
-    copy = swap(ybuf, ygot, 6)
-    copy.wait()
 
     loss_acc[...] = jnp.zeros((8, LANES), f32)
 
@@ -353,10 +359,13 @@
         fill_stack(q, (2.0 / CHANNELS) * residual * weight)
         return carry
 
-    lax.fori_loop(0, 16, predict, 0)
+    copies[0].wait()
+    lax.fori_loop(0, 8, predict, 0)
+    copies[1].wait()
+    lax.fori_loop(8, 16, predict, 0)
 
     def send_predicted(step, carry):
-        to = (step + at) % 32
+        to = (step + at + 14) % 32
         deliver(
             pbuf.at[to, own_half], pred_out.at[owner_row, own_half], 7, 2 * plane + owner_core, to
         )
@@ -374,10 +383,26 @@
     real, imag = forward()
     across_r = (real * spec_x[0] + imag * spec_x[1]) * factor
     across_i = (imag * spec_x[0] - real * spec_x[1]) * factor
-    local = inverse(across_r, across_i)
-    c_lin[pl.ds(0, N1, stride=2), :] = local[:, :LANES]
-    c_lin[pl.ds(1, N1, stride=2), :] = local[:, LANES:]
-    copy = swap(cbuf.at[:, pl.ds(2 * (1 - core), 2)], cgot, 9)
+    copies = []
+
+    def exchange_grad(half, value):
+        base, place = half * N1, pl.ds(half * 4, 4)
+        c_lin[pl.ds(base, HALF, stride=2), :] = value[:, :LANES]
+        c_lin[pl.ds(base + 1, HALF, stride=2), :] = value[:, LANES:]
+        copies.append(swap(cbuf.at[place, pl.ds(2 * (1 - core), 2)], cgot.at[place], 9 + 7 * half))
+
+    inverse(across_r, across_i, exchange_grad)
+
+    for half in (0, 1):
+        copies[half].wait()
+        place = pl.ds(half * 4, 4)
+        csum[place] = cbuf[place, pl.ds(2 * core, 2)] + cgot[place]
+        for far in FAR_FIRST:
+            to = (plane + far) % 8
+            piece = pl.ds(pl.multiple_of((to // 2) * 8, 8), 8)
+            deliver(
+                csum.at[place, to % 2, piece], along_y.at[half, plane], 11 + 6 * half, 2 * to + core, at
+            )
 
     arrived(loss_mid, 8)
     loss_sum[...] = jnp.sum(loss_mid[...], axis=0)
@@ -387,38 +412,25 @@
         return carry
 
     lax.fori_loop(0, 32, send_loss_sum, 0)
-    copy.wait()
-    csum[...] = cbuf[:, pl.ds(2 * core, 2)] + cgot[...]
-
-    def send_along(step, carry):
-        to = (plane + step) % 8
-        piece = pl.ds(pl.multiple_of((to // 2) * 8, 8), 8)
-        deliver(csum.at[:, to % 2, piece], along_y.at[plane], 11, 2 * to + core, at)
-        return carry
-
-    lax.fori_loop(0, 8, send_along, 0)
-    arrived(along_y, 11)
-    along_sum[...] = jnp.sum(along_y[...], axis=0)
-
-    def send_across(step, carry):
-        deliver(
-            along_sum.at[step], across.at[owner_row // 2, owner_core], 12,
-            2 * plane + row_odd, 4 * step + 2 * core + on_plane,
-        )
-        return carry
-
-    lax.fori_loop(0, 8, send_across, 0)
+
+    for half in (0, 1):
+        arrived(along_y.at[half], 11 + 6 * half)
+        along_sum[pl.ds(half * 4, 4)] = jnp.sum(along_y[half], axis=0)
+        for step in range(half * 4, half * 4 + 4):
+            deliver(
+                along_sum.at[step], across.at[owner_row // 2, owner_core], 12,
+                2 * plane + row_odd, 4 * step + 2 * core + on_plane,
+            )
 
     @pl.when(active)
     def _():
         arrived(across, 12)
         across_sum[...] = across[:, 0] + across[:, 1]
 
-        def send_total(step, carry):
-            deliver(across_sum, grad_out.at[:, core, own_piece], 13, 2 * ((plane + step) % 8) + core, at)
-            return carry
-
-        lax.fori_loop(0, 8, send_total, 0)
+        for far in FAR_FIRST:
+            deliver(
+                across_sum, grad_out.at[:, core, own_piece], 13, 2 * ((plane + far) % 8) + core, at
+            )
 
     arrived(loss_all, 10)
     everything = jnp.sum(jnp.sum(loss_all[...], axis=0), keepdims=True)
@@ -451,7 +463,8 @@
     drain(own_core, xbuf.at[:, pl.ds(0, 16)], xbuf.at[pl.ds(0, 31), pl.ds(0, 16)], 7)
     sent(loss_mid.at[pl.ds(0, 7)], 8)
     sent(loss_all.at[pl.ds(0, 31)], 10)
-    sent(xbuf.at[pl.ds(0, 14)], 11)
+    sent(xbuf.at[pl.ds(0, 7)], 11)
+    sent(xbuf.at[pl.ds(0, 7)], 17)
     drain(
         jnp.logical_and(active, row_odd == core), along_sum, along_sum.at[pl.ds(0, 7)], 12
     )
@@ -480,7 +493,7 @@
             space(512, LANES), space(512, LANES), space(8, LANES), space(8, LANES),
             space(SHARDS, SEGS, LANES), space(8, 4, SEGS, LANES), space(SHARDS, SEGS, LANES),
             space(N1, N2), space(N1, N2), space(8, 4, SEGS, LANES), space(8, 2, SEGS, LANES),
-            space(8, 2, SEGS, LANES), space(8, 8, 8, LANES), space(8, 8, LANES),
+            space(8, 2, SEGS, LANES), space(2, 8, 4, 8, LANES), space(8, 8, LANES),
             space(8, 2, 8, LANES), space(8, 8, LANES),
             space(8, LANES), space(1, LANES), space(8, 1, LANES), space(1, LANES), space(32, 1, LANES),
             space(N1, 3 * N1, kind=bf16), space(N1, 3 * N1, kind=bf16), space(3 * N2, 2 * N2, kind=bf16),
@@ -489,7 +502,7 @@
             space(N2, N2, kind=bf16), space(N1, N1, kind=bf16), space(N1, N2),
             space(N1, N2), space(N1, N2), space(N1, N2), space(3 * N1, N2, kind=bf16),
             space(N1, 3 * N2, kind=bf16), space(2, HALF, N2),
-            pltpu.SemaphoreType.DMA((10,)), pltpu.SemaphoreType.DMA((15,)), pltpu.SemaphoreType.DMA((15,)),
+            pltpu.SemaphoreType.DMA((10,)), pltpu.SemaphoreType.DMA((18,)), pltpu.SemaphoreType.DMA((18,)),
         ],
         compiler_params=pltpu.CompilerParams(has_side_effects=True, collective_id=1),
     )(

time: 81.2 us -> 70.6 us (0.87)
  Pallas kernels: 76.5 us -> 65.9 us
    pallas_call x1, Pallas kernels: 76.5 us -> 65.9 us  [per_device(): pl.pallas_call(kernel, out_shape=(jax.ShapeDtypeStruct((16, SEGS, LANES),...]
where the time goes in v3:
time: 70.6 us; the launch traced here: 70.4 us
  Pallas kernels  65.9 us (93%)
  between operations  2.4 us (3%)
  local copies, waits for them, and re-layouts  2.12 us (3%)
    pallas_call x1, Pallas kernels, per_device(): pl.pallas_call(kernel, out_shape=(jax.ShapeDtypeStruct((16, SEGS, LANES),...  65.9 us
    reshape x1, local copies, waits for them, and re-layouts, per_device(): grad.reshape(16, 4096)  2.12 us

profile of v3, /device:TPU:1, one launch (start us, length us, event | category | flops | bytes accessed | tf_op | source)
XLA Modules:
  0.0 70.4 jit_solution(13440106796251517666)
XLA Ops:
  0.6 65.9 %shard_map.139 = (f32[16,32,128]{2,1,0:T(8,128)}, f32[8,2,32,128]{3,2,1,0:T(8,128)}, f32[1,1]{1,0:T(1,128)}) custom-call(f32[16,4096]{1,0:T(8,128)} %signal.1, f32[16,4096]{1,0:T(8,128)} %filters.1, f32[1,16]{1,0:T(1,128)} %bitcast.12, f32[1,16]{1,0:T(1,128)} %bitcast.13, bf16[512,512]{1,0:T(8,128)(2,1)} %constant.16.clone.outer_h, ...), custom_call_target="tpu_custom_call" | custom-call | tf_op jit(solution)/shard_map/pallas_call | solution.py:483
  66.5 2.1 %copy_bitcast_fusion = (f32[16,4096]{1,0:T(8,128)}, f32[16,4096]{1,0:T(8,128)}) fusion(f32[2,8,32,128]{3,2,1,0:T(8,128)} %bitcast.11, f32[2,8,32,128]{3,2,1,0:T(8,128)} %bitcast.10), kind=kLoop, calls=%fused_computation | loop fusion | bytes 1048576 | tf_op jit(solution)/shard_map/reshape | solution.py:512

commit v4 on v3

--- a/solution.py
+++ b/solution.py
@@ -59,10 +59,10 @@
 
 
 def kernel(
-    signal, filters, scale_in, shift_in,
+    signal_hbm, filters_hbm, scale_in, shift_in,
     outer_h, outer_l, outer_th, outer_tl, inner_h, inner_l, twist_hbm, lane_ref,
     pred_out, grad_out, loss_out,
-    signal_send, filter_send, gate_send, gate_got,
+    signal, filters, signal_send, filter_send, gate_send, gate_got,
     xbuf, fbuf, pbuf, ybuf, ygot, cbuf, cgot, csum, along_y, along_sum, across, across_sum,
     loss_acc, loss_own, loss_mid, loss_sum, loss_all,
     outer_k, outer_tk, inner_k, twist,
@@ -83,22 +83,18 @@
 
     barrier = pltpu.get_barrier_semaphore()
 
-    def greet(step, carry):
-        other = (core * SHARDS + at + step) % (2 * SHARDS)
-        pl.semaphore_signal(
-            barrier, inc=1, device_id=(2 * plane + other // SHARDS, other % SHARDS), device_id_type=MESH
-        )
-        return carry
-
-    lax.fori_loop(1, 2 * SHARDS, greet, 0)
-
-    def greet_planes(step, carry):
-        pl.semaphore_signal(
-            barrier, inc=1, device_id=(2 * ((plane + step) % 8) + core, at), device_id_type=MESH
-        )
-        return carry
-
-    lax.fori_loop(1, 8, greet_planes, 0)
+    def greet(chan, tm):
+        pl.semaphore_signal(barrier, inc=1, device_id=(chan, tm), device_id_type=MESH)
+
+    for far in FAR_FIRST[:-1]:
+        for step in range(8):
+            greet(2 * plane + step % 2, 4 * ((depth + far) % 8) + step // 2)
+    for far in FAR_FIRST[:-1]:
+        greet(2 * ((plane + far) % 8) + core, at)
+    for side in (2, 1, 3):
+        for step in (0, 1):
+            greet(2 * plane + step, 4 * depth + (width + side) % 4)
+    greet(partner, at)
 
     def fetch(source, target, number):
         return pltpu.make_async_copy(source, target, table_sem.at[number])
@@ -112,6 +108,10 @@
         (inner_l, inner_k.at[pl.ds(2 * N2, N2)]),
         (twist_hbm, twist),
     ]
+    own_taps = pl.ds(pl.multiple_of((plane // 2) * 1024, 1024), 1024)
+    inputs = [(signal_hbm, signal), (filters_hbm.at[:, own_taps], filters)]
+    for number, (source, target) in enumerate(inputs):
+        fetch(source, target, 10 + number).start()
     for number, (source, target) in enumerate(tables):
         fetch(source, target, number).start()
 
@@ -143,29 +143,21 @@
         copy.start()
         return copy
 
-    for seg in range(SEGS):
-        signal_send[pl.ds(seg, 16, stride=SEGS), :] = signal[:, seg * LANES : (seg + 1) * LANES]
+    def signal_turn(seg, carry):
+        signal_send[pl.ds(seg, 16, stride=SEGS), :] = signal[:, pl.ds(pl.multiple_of(seg * LANES, LANES), LANES)]
+        return carry
+
+    fetch(*inputs[0], 10).wait()
+    lax.fori_loop(0, SEGS, signal_turn, 0, unroll=4)
     signal_rows = signal_send.reshape(16, SEGS, LANES)
     gate_send[...] = jnp.zeros((8, LANES), f32)
     gate_send[0:1, 0:16] = scale_in[...]
     gate_send[1:2, 0:16] = shift_in[...]
-    for seg in range(SEGS):
-        filter_send[pl.ds(seg, 16, stride=SEGS), :] = filters[:, seg * LANES : (seg + 1) * LANES]
-    filter_rows = filter_send.reshape(16, SEGS, LANES)
-    row_up = lax.broadcasted_iota(jnp.int32, (N2, N2), 0)
-    col_up = lax.broadcasted_iota(jnp.int32, (N2, N2), 1)
-    tri_up[...] = jnp.where(row_up <= col_up, 1.0, 0.0).astype(bf16)
-    def rows(q, offset=0):
-        return pl.ds(pl.multiple_of(q * 32 + offset, 32), 32)
-
-    row_low = lax.broadcasted_iota(jnp.int32, (32, N1), 0)
-    col_low = lax.broadcasted_iota(jnp.int32, (32, N1), 1)
-
-    def fill_low(q, carry):
-        tri_low[rows(q), :] = jnp.where(col_low < row_low + q * 32, 1.0, 0.0).astype(bf16)
-        return carry
-
-    lax.fori_loop(0, 16, fill_low, 0)
+    fetch(*inputs[1], 11).wait()
+    for seg in range(8):
+        filter_send[pl.ds(seg, 16, stride=8), :] = filters[:, seg * LANES : (seg + 1) * LANES]
+    filter_rows = filter_send.reshape(16, 8, LANES)
+
     pl.semaphore_wait(barrier, 2 * SHARDS - 1 + 7)
 
     @pl.when(active)
@@ -174,7 +166,7 @@
             for side in (0, 1):
                 row = 2 * ((depth + far) % 8) + side
                 deliver(
-                    filter_rows.at[row, own_piece], fbuf.at[depth, width, own_piece], 2,
+                    filter_rows.at[row], fbuf.at[depth, width, own_piece], 2,
                     2 * plane + row_odd, 2 * row + core,
                 )
 
@@ -187,6 +179,22 @@
                     signal_rows.at[row, part], xbuf.at[at, part], 0, 2 * plane + half, 2 * row + core
                 )
     gates = swap(gate_send, gate_got, 1)
+
+    row_up = lax.broadcasted_iota(jnp.int32, (N2, N2), 0)
+    col_up = lax.broadcasted_iota(jnp.int32, (N2, N2), 1)
+    tri_up[...] = jnp.where(row_up <= col_up, 1.0, 0.0).astype(bf16)
+
+    def rows(q, offset=0):
+        return pl.ds(pl.multiple_of(q * 32 + offset, 32), 32)
+
+    row_low = lax.broadcasted_iota(jnp.int32, (32, N1), 0)
+    col_low = lax.broadcasted_iota(jnp.int32, (32, N1), 1)
+
+    def fill_low(q, carry):
+        tri_low[rows(q), :] = jnp.where(col_low < row_low + q * 32, 1.0, 0.0).astype(bf16)
+        return carry
+
+    lax.fori_loop(0, 16, fill_low, 0)
 
     for number, (source, target) in enumerate(tables):
         fetch(source, target, number).wait()
@@ -273,7 +281,7 @@
             triple_q[rows(q, part * N1), :] = piece
         return carry
 
-    lax.fori_loop(0, 16, split_rows, 0)
+    lax.fori_loop(0, 16, split_rows, 0, unroll=2)
     sums = dot(triple_x[...], tri_up[...])
     normed_s[...] = sums[:N1] + sums[N1 : 2 * N1] + sums[2 * N1 :]
     sums = dot(triple_q[...], tri_up[...])
@@ -312,7 +320,7 @@
         fill_stack(q, normed)
         return carry
 
-    lax.fori_loop(0, 16, normalize, 0)
+    lax.fori_loop(0, 16, normalize, 0, unroll=2)
     arrived(xbuf.at[pl.ds(0, 14)], 3)
     core_blocks = fbuf.at[:, pl.ds(2 * core, 2)]
     copy = swap(core_blocks, core_blocks, 5)
@@ -324,7 +332,7 @@
         fill_stack(q, pair_rows(f_lin, q))
         return carry
 
-    lax.fori_loop(0, 16, take_filter, 0)
+    lax.fori_loop(0, 16, take_filter, 0, unroll=2)
     real, imag = forward()
     factor = 1.0 / math.sqrt(LENGTH) / LENGTH
     real, imag = real * factor, imag * factor
@@ -360,25 +368,9 @@
         return carry
 
     copies[0].wait()
-    lax.fori_loop(0, 8, predict, 0)
+    lax.fori_loop(0, 8, predict, 0, unroll=2)
     copies[1].wait()
-    lax.fori_loop(8, 16, predict, 0)
-
-    def send_predicted(step, carry):
-        to = (step + at + 14) % 32
-        deliver(
-            pbuf.at[to, own_half], pred_out.at[owner_row, own_half], 7, 2 * plane + owner_core, to
-        )
-        return carry
-
-    lax.fori_loop(0, 32, send_predicted, 0)
-    loss_own[...] = jnp.sum(loss_acc[...], axis=0, keepdims=True)
-
-    def send_loss(step, carry):
-        deliver(loss_own, loss_mid.at[plane], 8, 2 * ((plane + step) % 8) + core, at)
-        return carry
-
-    lax.fori_loop(0, 8, send_loss, 0)
+    lax.fori_loop(8, 16, predict, 0, unroll=2)
 
     real, imag = forward()
     across_r = (real * spec_x[0] + imag * spec_x[1]) * factor
@@ -403,6 +395,23 @@
             deliver(
                 csum.at[place, to % 2, piece], along_y.at[half, plane], 11 + 6 * half, 2 * to + core, at
             )
+
+    loss_own[...] = jnp.sum(loss_acc[...], axis=0, keepdims=True)
+
+    def send_loss(step, carry):
+        deliver(loss_own, loss_mid.at[plane], 8, 2 * ((plane + step) % 8) + core, at)
+        return carry
+
+    lax.fori_loop(0, 8, send_loss, 0)
+
+    def send_predicted(step, carry):
+        to = (step + at + 14) % 32
+        deliver(
+            pbuf.at[to, own_half], pred_out.at[owner_row, own_half], 7, 2 * plane + owner_core, to
+        )
+        return carry
+
+    lax.fori_loop(0, 32, send_predicted, 0)
 
     arrived(loss_mid, 8)
     loss_sum[...] = jnp.sum(loss_mid[...], axis=0)
@@ -483,14 +492,14 @@
     predicted, grad, loss = pl.pallas_call(
         kernel,
         out_shape=(
-            jax.ShapeDtypeStruct((16, SEGS, LANES), f32),
-            jax.ShapeDtypeStruct((8, 2, SEGS, LANES), f32),
+            pltpu.VMEM((16, SEGS, LANES), f32),
+            pltpu.VMEM((8, 2, SEGS, LANES), f32),
             jax.ShapeDtypeStruct((1, 1), f32),
         ),
-        in_specs=[vmem] * 4 + [anywhere] * 7 + [vmem],
-        out_specs=(anywhere, anywhere, vmem),
+        in_specs=[anywhere] * 2 + [vmem] * 2 + [anywhere] * 7 + [vmem],
+        out_specs=(vmem, vmem, vmem),
         scratch_shapes=[
-            space(512, LANES), space(512, LANES), space(8, LANES), space(8, LANES),
+            space(16, 4096), space(16, 1024), space(512, LANES), space(128, LANES), space(8, LANES), space(8, LANES),
             space(SHARDS, SEGS, LANES), space(8, 4, SEGS, LANES), space(SHARDS, SEGS, LANES),
             space(N1, N2), space(N1, N2), space(8, 4, SEGS, LANES), space(8, 2, SEGS, LANES),
             space(8, 2, SEGS, LANES), space(2, 8, 4, 8, LANES), space(8, 8, LANES),
@@ -502,7 +511,7 @@
             space(N2, N2, kind=bf16), space(N1, N1, kind=bf16), space(N1, N2),
             space(N1, N2), space(N1, N2), space(N1, N2), space(3 * N1, N2, kind=bf16),
             space(N1, 3 * N2, kind=bf16), space(2, HALF, N2),
-            pltpu.SemaphoreType.DMA((10,)), pltpu.SemaphoreType.DMA((18,)), pltpu.SemaphoreType.DMA((18,)),
+            pltpu.SemaphoreType.DMA((12,)), pltpu.SemaphoreType.DMA((18,)), pltpu.SemaphoreType.DMA((18,)),
         ],
         compiler_params=pltpu.CompilerParams(has_side_effects=True, collective_id=1),
     )(

time: 70.6 us -> 71.1 us (level)
  Pallas kernels: 65.9 us -> 67.4 us
  local copies, waits for them, and re-layouts: 2.12 us -> 1.1 us
    pallas_call x1, Pallas kernels: 65.9 us -> 67.4 us  [per_device(): pl.pallas_call(kernel, out_shape=(pltpu.VMEM((16, SEGS, LANES), f32), plt...]
    reshape x1, local copies, waits for them, and re-layouts: 2.12 us -> 1.1 us  [per_device(): grad.reshape(16, 4096)]
where the time goes in v4:
time: 71.1 us; the launch traced here: 70.9 us
  Pallas kernels  67.4 us (95%)
  between operations  2.4 us (3%)
  local copies, waits for them, and re-layouts  1.1 us (2%)
    pallas_call x1, Pallas kernels, per_device(): pl.pallas_call(kernel, out_shape=(pltpu.VMEM((16, SEGS, LANES), f32), plt...  67.4 us

profile of v4, /device:TPU:1, one launch (start us, length us, event | category | flops | bytes accessed | tf_op | source)
XLA Modules:
  0.0 70.9 jit_solution(16504048982664052529)
XLA Ops:
  0.6 67.4 %shard_map.139 = (f32[16,32,128]{2,1,0:T(8,128)S(1)}, f32[8,2,32,128]{3,2,1,0:T(8,128)S(1)}, f32[1,1]{1,0:T(1,128)}) custom-call(f32[16,4096]{1,0:T(8,128)} %signal_hbm.1, f32[16,4096]{1,0:T(8,128)} %filters_hbm.1, f32[1,16]{1,0:T(1,128)} %bitcast.12, f32[1,16]{1,0:T(1,128)} %bitcast.13, bf16[512,512]{1,0:T(8,128)(2,1)} %constant.16.clone.outer_h, ...), custom_call_target="tpu_custom_call" | custom-call | tf_op jit(solution)/shard_map/pallas_call | solution.py:492
  68.1 1.1 %copy_bitcast_fusion = (f32[16,4096]{1,0:T(8,128)}, f32[16,4096]{1,0:T(8,128)}) fusion(f32[2,8,32,128]{3,2,1,0:T(8,128)S(1)} %bitcast.11, f32[2,8,32,128]{3,2,1,0:T(8,128)S(1)} %bitcast.10), kind=kLoop, calls=%fused_computation | loop fusion | bytes 1048576 | tf_op jit(solution)/shard_map/reshape | solution.py:521

commit v5 on v4

--- a/solution.py
+++ b/solution.py
@@ -132,6 +132,12 @@
         def _():
             pltpu.make_async_copy(source, target, recv_sem.at[number]).start()
 
+    def deliver_far(far, source, target, number, chan, tm):
+        if far:
+            remote(source, target, number, chan, tm).start()
+        else:
+            deliver(source, target, number, chan, tm)
+
     def arrived(target, number):
         pltpu.make_async_copy(target, target, recv_sem.at[number]).wait()
 
@@ -165,8 +171,8 @@
         for far in FAR_FIRST:
             for side in (0, 1):
                 row = 2 * ((depth + far) % 8) + side
-                deliver(
-                    filter_rows.at[row], fbuf.at[depth, width, own_piece], 2,
+                deliver_far(
+                    far, filter_rows.at[row], fbuf.at[depth, width, own_piece], 2,
                     2 * plane + row_odd, 2 * row + core,
                 )
 
@@ -175,8 +181,8 @@
             row = 2 * ((depth + far) % 8) + side
             for half in (0, 1):
                 part = pl.ds(half * 16, 16)
-                deliver(
-                    signal_rows.at[row, part], xbuf.at[at, part], 0, 2 * plane + half, 2 * row + core
+                deliver_far(
+                    far, signal_rows.at[row, part], xbuf.at[at, part], 0, 2 * plane + half, 2 * row + core
                 )
     gates = swap(gate_send, gate_got, 1)
 
@@ -372,6 +378,22 @@
     copies[1].wait()
     lax.fori_loop(8, 16, predict, 0, unroll=2)
 
+    loss_own[...] = jnp.sum(loss_acc[...], axis=0, keepdims=True)
+
+    def send_loss(step, carry):
+        deliver(loss_own, loss_mid.at[plane], 8, 2 * ((plane + step) % 8) + core, at)
+        return carry
+
+    lax.fori_loop(0, 8, send_loss, 0)
+
+    for far in FAR_FIRST:
+        for side in (2, 1, 3, 0):
+            to = 4 * ((depth + far) % 8) + (width + side) % 4
+            deliver_far(
+                far + side, pbuf.at[to, own_half], pred_out.at[owner_row, own_half], 7,
+                2 * plane + owner_core, to,
+            )
+
     real, imag = forward()
     across_r = (real * spec_x[0] + imag * spec_x[1]) * factor
     across_i = (imag * spec_x[0] - real * spec_x[1]) * factor
@@ -392,26 +414,9 @@
         for far in FAR_FIRST:
             to = (plane + far) % 8
             piece = pl.ds(pl.multiple_of((to // 2) * 8, 8), 8)
-            deliver(
-                csum.at[place, to % 2, piece], along_y.at[half, plane], 11 + 6 * half, 2 * to + core, at
+            deliver_far(
+                far, csum.at[place, to % 2, piece], along_y.at[half, plane], 11 + 6 * half, 2 * to + core, at
             )
-
-    loss_own[...] = jnp.sum(loss_acc[...], axis=0, keepdims=True)
-
-    def send_loss(step, carry):
-        deliver(loss_own, loss_mid.at[plane], 8, 2 * ((plane + step) % 8) + core, at)
-        return carry
-
-    lax.fori_loop(0, 8, send_loss, 0)
-
-    def send_predicted(step, carry):
-        to = (step + at + 14) % 32
-        deliver(
-            pbuf.at[to, own_half], pred_out.at[owner_row, own_half], 7, 2 * plane + owner_core, to
-        )
-        return carry
-
-    lax.fori_loop(0, 32, send_predicted, 0)
 
     arrived(loss_mid, 8)
     loss_sum[...] = jnp.sum(loss_mid[...], axis=0)
@@ -437,8 +442,8 @@
         across_sum[...] = across[:, 0] + across[:, 1]
 
         for far in FAR_FIRST:
-            deliver(
-                across_sum, grad_out.at[:, core, own_piece], 13, 2 * ((plane + far) % 8) + core, at
+            deliver_far(
+                far, across_sum, grad_out.at[:, core, own_piece], 13, 2 * ((plane + far) % 8) + core, at
             )
 
     arrived(loss_all, 10)

time: 71.1 us -> 67.2 us (0.945)
  Pallas kernels: 67.4 us -> 63.5 us
    pallas_call x1, Pallas kernels: 67.4 us -> 63.5 us  [per_device(): pl.pallas_call(kernel, out_shape=(pltpu.VMEM((16, SEGS, LANES), f32), plt...]
where the time goes in v5:
time: 67.2 us; the launch traced here: 67 us
  Pallas kernels  63.5 us (94%)
  between operations  2.4 us (4%)
  local copies, waits for them, and re-layouts  1.1 us (2%)
    pallas_call x1, Pallas kernels, per_device(): pl.pallas_call(kernel, out_shape=(pltpu.VMEM((16, SEGS, LANES), f32), plt...  63.5 us

profile of v5, /device:TPU:1, one launch (start us, length us, event | category | flops | bytes accessed | tf_op | source)
XLA Modules:
  0.0 67.0 jit_solution(4905328227707449609)
XLA Ops:
  0.6 63.5 %shard_map.139 = (f32[16,32,128]{2,1,0:T(8,128)S(1)}, f32[8,2,32,128]{3,2,1,0:T(8,128)S(1)}, f32[1,1]{1,0:T(1,128)}) custom-call(f32[16,4096]{1,0:T(8,128)} %signal_hbm.1, f32[16,4096]{1,0:T(8,128)} %filters_hbm.1, f32[1,16]{1,0:T(1,128)} %bitcast.12, f32[1,16]{1,0:T(1,128)} %bitcast.13, bf16[512,512]{1,0:T(8,128)(2,1)} %constant.16.clone.outer_h, ...), custom_call_target="tpu_custom_call" | custom-call | tf_op jit(solution)/shard_map/pallas_call | solution.py:497
  64.2 1.1 %copy_bitcast_fusion = (f32[16,4096]{1,0:T(8,128)}, f32[16,4096]{1,0:T(8,128)}) fusion(f32[2,8,32,128]{3,2,1,0:T(8,128)S(1)} %bitcast.11, f32[2,8,32,128]{3,2,1,0:T(8,128)S(1)} %bitcast.10), kind=kLoop, calls=%fused_computation | loop fusion | bytes 1048576 | tf_op jit(solution)/shard_map/reshape | solution.py:526

commit v6 on v5

--- a/solution.py
+++ b/solution.py
@@ -59,10 +59,10 @@
 
 
 def kernel(
-    signal_hbm, filters_hbm, scale_in, shift_in,
-    outer_h, outer_l, outer_th, outer_tl, inner_h, inner_l, twist_hbm, lane_ref,
+    signal_hbm, filters_hbm, scale_hbm, shift_hbm,
+    outer_h, outer_l, outer_th, outer_tl, inner_h, inner_l, twist_hbm, lane_hbm,
     pred_out, grad_out, loss_out,
-    signal, filters, signal_send, filter_send, gate_send, gate_got,
+    signal, filters, scale_in, shift_in, lane_ref, signal_send, filter_send, gate_send, gate_got,
     xbuf, fbuf, pbuf, ybuf, ygot, cbuf, cgot, csum, along_y, along_sum, across, across_sum,
     loss_acc, loss_own, loss_mid, loss_sum, loss_all,
     outer_k, outer_tk, inner_k, twist,
@@ -106,12 +106,12 @@
         (outer_tl, outer_tk.at[:, pl.ds(2 * N1, N1)]),
         (inner_h, inner_k.at[pl.ds(0, N2)]), (inner_h, inner_k.at[pl.ds(N2, N2)]),
         (inner_l, inner_k.at[pl.ds(2 * N2, N2)]),
-        (twist_hbm, twist),
+        (twist_hbm, twist), (lane_hbm, lane_ref), (scale_hbm, scale_in), (shift_hbm, shift_in),
     ]
     own_taps = pl.ds(pl.multiple_of((plane // 2) * 1024, 1024), 1024)
     inputs = [(signal_hbm, signal), (filters_hbm.at[:, own_taps], filters)]
     for number, (source, target) in enumerate(inputs):
-        fetch(source, target, 10 + number).start()
+        fetch(source, target, 13 + number).start()
     for number, (source, target) in enumerate(tables):
         fetch(source, target, number).start()
 
@@ -153,13 +153,10 @@
         signal_send[pl.ds(seg, 16, stride=SEGS), :] = signal[:, pl.ds(pl.multiple_of(seg * LANES, LANES), LANES)]
         return carry
 
-    fetch(*inputs[0], 10).wait()
+    fetch(*inputs[0], 13).wait()
     lax.fori_loop(0, SEGS, signal_turn, 0, unroll=4)
     signal_rows = signal_send.reshape(16, SEGS, LANES)
-    gate_send[...] = jnp.zeros((8, LANES), f32)
-    gate_send[0:1, 0:16] = scale_in[...]
-    gate_send[1:2, 0:16] = shift_in[...]
-    fetch(*inputs[1], 11).wait()
+    fetch(*inputs[1], 14).wait()
     for seg in range(8):
         filter_send[pl.ds(seg, 16, stride=8), :] = filters[:, seg * LANES : (seg + 1) * LANES]
     filter_rows = filter_send.reshape(16, 8, LANES)
@@ -184,8 +181,6 @@
                 deliver_far(
                     far, signal_rows.at[row, part], xbuf.at[at, part], 0, 2 * plane + half, 2 * row + core
                 )
-    gates = swap(gate_send, gate_got, 1)
-
     row_up = lax.broadcasted_iota(jnp.int32, (N2, N2), 0)
     col_up = lax.broadcasted_iota(jnp.int32, (N2, N2), 1)
     tri_up[...] = jnp.where(row_up <= col_up, 1.0, 0.0).astype(bf16)
@@ -204,6 +199,10 @@
 
     for number, (source, target) in enumerate(tables):
         fetch(source, target, number).wait()
+    gate_send[...] = jnp.zeros((8, LANES), f32)
+    gate_send[0:1, 0:16] = scale_in[...]
+    gate_send[1:2, 0:16] = shift_in[...]
+    gates = swap(gate_send, gate_got, 1)
     core_f = core.astype(f32)
     lane_r = 1.0 + core_f * (lane_ref[0:1, :] - 1.0)
     lane_i = core_f * lane_ref[1:2, :]
@@ -326,7 +325,7 @@
         fill_stack(q, normed)
         return carry
 
-    lax.fori_loop(0, 16, normalize, 0, unroll=2)
+    lax.fori_loop(0, 16, normalize, 0, unroll=4)
     arrived(xbuf.at[pl.ds(0, 14)], 3)
     core_blocks = fbuf.at[:, pl.ds(2 * core, 2)]
     copy = swap(core_blocks, core_blocks, 5)
@@ -374,9 +373,9 @@
         return carry
 
     copies[0].wait()
-    lax.fori_loop(0, 8, predict, 0, unroll=2)
+    lax.fori_loop(0, 8, predict, 0, unroll=4)
     copies[1].wait()
-    lax.fori_loop(8, 16, predict, 0, unroll=2)
+    lax.fori_loop(8, 16, predict, 0, unroll=4)
 
     loss_own[...] = jnp.sum(loss_acc[...], axis=0, keepdims=True)
 
@@ -499,12 +498,13 @@
         out_shape=(
             pltpu.VMEM((16, SEGS, LANES), f32),
             pltpu.VMEM((8, 2, SEGS, LANES), f32),
-            jax.ShapeDtypeStruct((1, 1), f32),
+            pltpu.VMEM((1, 1), f32),
         ),
-        in_specs=[anywhere] * 2 + [vmem] * 2 + [anywhere] * 7 + [vmem],
+        in_specs=[anywhere] * 12,
         out_specs=(vmem, vmem, vmem),
         scratch_shapes=[
-            space(16, 4096), space(16, 1024), space(512, LANES), space(128, LANES), space(8, LANES), space(8, LANES),
+            space(16, 4096), space(16, 1024), space(1, 16), space(1, 16), space(8, N2),
+            space(512, LANES), space(128, LANES), space(8, LANES), space(8, LANES),
             space(SHARDS, SEGS, LANES), space(8, 4, SEGS, LANES), space(SHARDS, SEGS, LANES),
             space(N1, N2), space(N1, N2), space(8, 4, SEGS, LANES), space(8, 2, SEGS, LANES),
             space(8, 2, SEGS, LANES), space(2, 8, 4, 8, LANES), space(8, 8, LANES),
@@ -516,7 +516,7 @@
             space(N2, N2, kind=bf16), space(N1, N1, kind=bf16), space(N1, N2),
             space(N1, N2), space(N1, N2), space(N1, N2), space(3 * N1, N2, kind=bf16),
             space(N1, 3 * N2, kind=bf16), space(2, HALF, N2),
-            pltpu.SemaphoreType.DMA((12,)), pltpu.SemaphoreType.DMA((18,)), pltpu.SemaphoreType.DMA((18,)),
+            pltpu.SemaphoreType.DMA((15,)), pltpu.SemaphoreType.DMA((18,)), pltpu.SemaphoreType.DMA((18,)),
         ],
         compiler_params=pltpu.CompilerParams(has_side_effects=True, collective_id=1),
     )(

time: 67.2 us -> 65.1 us (0.969)
  Pallas kernels: 63.5 us -> 62.1 us
    pallas_call x1, Pallas kernels: 63.5 us -> 62.1 us  [per_device(): pl.pallas_call(kernel, out_shape=(pltpu.VMEM((16, SEGS, LANES), f32), plt...]
where the time goes in v6:
time: 65.1 us; the launch traced here: 65 us
  Pallas kernels  62.1 us (95%)
  between operations  1.8 us (3%)
  local copies, waits for them, and re-layouts  1.1 us (2%)
    pallas_call x1, Pallas kernels, per_device(): pl.pallas_call(kernel, out_shape=(pltpu.VMEM((16, SEGS, LANES), f32), plt...  62.1 us

profile of v6, /device:TPU:1, one launch (start us, length us, event | category | flops | bytes accessed | tf_op | source)
XLA Modules:
  0.0 65.0 jit_solution(18273122618546703234)
XLA Ops:
  0.6 62.1 %shard_map.139 = (f32[16,32,128]{2,1,0:T(8,128)S(1)}, f32[8,2,32,128]{3,2,1,0:T(8,128)S(1)}, f32[1,1]{1,0:T(1,128)S(1)}) custom-call(f32[16,4096]{1,0:T(8,128)} %signal_hbm.1, f32[16,4096]{1,0:T(8,128)} %filters_hbm.1, f32[1,16]{1,0:T(1,128)} %bitcast.12, f32[1,16]{1,0:T(1,128)} %bitcast.13, bf16[512,512]{1,0:T(8,128)(2,1)} %constant.16.clone.outer_h, ...), custom_call_target="tpu_custom_call" | custom-call | tf_op jit(solution)/shard_map/pallas_call | solution.py:496
  62.8 1.1 %copy_bitcast_fusion = (f32[16,4096]{1,0:T(8,128)}, f32[16,4096]{1,0:T(8,128)}) fusion(f32[2,8,32,128]{3,2,1,0:T(8,128)S(1)} %bitcast.11, f32[2,8,32,128]{3,2,1,0:T(8,128)S(1)} %bitcast.10), kind=kLoop, calls=%fused_computation | loop fusion | bytes 1048576 | tf_op jit(solution)/shard_map/reshape | solution.py:526

commit v7 on v6

--- a/solution.py
+++ b/solution.py
@@ -439,18 +439,22 @@
     def _():
         arrived(across, 12)
         across_sum[...] = across[:, 0] + across[:, 1]
+        own_sem = 18 + plane // 2
 
         for far in FAR_FIRST:
             deliver_far(
-                far, across_sum, grad_out.at[:, core, own_piece], 13, 2 * ((plane + far) % 8) + core, at
+                far, across_sum, grad_out.at[:, core, own_piece], own_sem, 2 * ((plane + far) % 8) + core, at
             )
 
     arrived(loss_all, 10)
     everything = jnp.sum(jnp.sum(loss_all[...], axis=0), keepdims=True)
     loss_out[...] = everything / (CHANNELS * (LENGTH - 1))
 
-    arrived(grad_out.at[:, core], 13)
-    copy = swap(grad_out.at[:, core], grad_out.at[:, core], 14)
+    forwarded = []
+    for piece in range(4):
+        place = grad_out.at[:, core, pl.ds(8 * piece, 8)]
+        arrived(place, 18 + piece)
+        forwarded.append(swap(place, place, 22 + piece))
 
     def drain(less, whole, part, number):
         @pl.when(less)
@@ -462,6 +466,7 @@
             sent(whole, number)
 
     own_core = owner_core == core
+    own_sem_all = 18 + plane // 2
     drain(own_core, xbuf.at[:, pl.ds(0, 16)], xbuf.at[pl.ds(0, 31), pl.ds(0, 16)], 0)
 
     @pl.when(active)
@@ -470,7 +475,7 @@
             jnp.logical_and(own_core, row_odd == core),
             xbuf.at[pl.ds(0, 16), pl.ds(0, 8)], xbuf.at[pl.ds(0, 15), pl.ds(0, 8)], 2,
         )
-        sent(xbuf.at[pl.ds(0, 14)], 13)
+        sent(xbuf.at[pl.ds(0, 14)], own_sem_all)
 
     sent(xbuf.at[pl.ds(0, 14)], 3)
     drain(own_core, xbuf.at[:, pl.ds(0, 16)], xbuf.at[pl.ds(0, 31), pl.ds(0, 16)], 7)
@@ -482,7 +487,8 @@
         jnp.logical_and(active, row_odd == core), along_sum, along_sum.at[pl.ds(0, 7)], 12
     )
     arrived(pred_out, 7)
-    copy.wait()
+    for copy in forwarded:
+        copy.wait()
 
 
 def per_device(signal, filters, gate_scale, gate_shift):
@@ -516,7 +522,7 @@
             space(N2, N2, kind=bf16), space(N1, N1, kind=bf16), space(N1, N2),
             space(N1, N2), space(N1, N2), space(N1, N2), space(3 * N1, N2, kind=bf16),
             space(N1, 3 * N2, kind=bf16), space(2, HALF, N2),
-            pltpu.SemaphoreType.DMA((15,)), pltpu.SemaphoreType.DMA((18,)), pltpu.SemaphoreType.DMA((18,)),
+            pltpu.SemaphoreType.DMA((15,)), pltpu.SemaphoreType.DMA((26,)), pltpu.SemaphoreType.DMA((26,)),
         ],
         compiler_params=pltpu.CompilerParams(has_side_effects=True, collective_id=1),
     )(

time: 65.1 us -> 65.1 us (level)
  no operation moved by 1% of the time
where the time goes in v7:
time: 65.1 us; the launch traced here: 65 us
  Pallas kernels  62.1 us (95%)
  between operations  1.8 us (3%)
  local copies, waits for them, and re-layouts  1.1 us (2%)
    pallas_call x1, Pallas kernels, per_device(): pl.pallas_call(kernel, out_shape=(pltpu.VMEM((16, SEGS, LANES), f32), plt...  62.1 us

profile of v7, /device:TPU:1, one launch (start us, length us, event | category | flops | bytes accessed | tf_op | source)
XLA Modules:
  0.0 65.0 jit_solution(13038981512401119900)
XLA Ops:
  0.6 62.1 %shard_map.139 = (f32[16,32,128]{2,1,0:T(8,128)S(1)}, f32[8,2,32,128]{3,2,1,0:T(8,128)S(1)}, f32[1,1]{1,0:T(1,128)S(1)}) custom-call(f32[16,4096]{1,0:T(8,128)} %signal_hbm.1, f32[16,4096]{1,0:T(8,128)} %filters_hbm.1, f32[1,16]{1,0:T(1,128)} %bitcast.12, f32[1,16]{1,0:T(1,128)} %bitcast.13, bf16[512,512]{1,0:T(8,128)(2,1)} %constant.16.clone.outer_h, ...), custom_call_target="tpu_custom_call" | custom-call | tf_op jit(solution)/shard_map/pallas_call | solution.py:502
  62.8 1.1 %copy_bitcast_fusion = (f32[16,4096]{1,0:T(8,128)}, f32[16,4096]{1,0:T(8,128)}) fusion(f32[2,8,32,128]{3,2,1,0:T(8,128)S(1)} %bitcast.11, f32[2,8,32,128]{3,2,1,0:T(8,128)S(1)} %bitcast.10), kind=kLoop, calls=%fused_computation | loop fusion | bytes 1048576 | tf_op jit(solution)/shard_map/reshape | solution.py:532
